TPU v7x, 512 devices: a whole 4x4x16 slice. The times are simulated.
512 devices in a mesh: freq: 128 (over x, z, core), bl: 4 (over y).
Axes of the slice: x: 4, y: 4, z: 16, core: 2. Of those that a mesh axis runs over, the one named last changes fastest.
Arguments:
- vis_time: bfloat16 [128, 2, 1024, 2048], P('freq', None, 'bl'), may hold values from -6 to 6
- owner: int32 [384, 1], replicated, may hold values from 0 to 127; in each aligned block of 384 rows (0 to 383, 384 to 767, ...) at most 4 rows name the same one
- counts: int32 [384, 128], replicated, may hold values from 1 to 4
- factors: bfloat16 [512, 128, 2, 4, 1024], P('freq', None, None, None, 'bl'), may hold values from -0.1875 to 0.1875
Outputs:
- filtered: bfloat16 [128, 2, 1024, 384], P('freq', None, 'bl')
Inputs may be any that keep to these rules, and one draw needn't show every extreme that they name: `owner`: every index of freq owns at least one m and at most 4; some index owns exactly 4.
All inputs are finite; a program needn't handle non-finite values.
Results may differ from a plain program's by a relative error of at most 0.0064.
Values may be sent and summed in bfloat16 or wider, within the bound.
No kernel may reach another device: no remote copies, remote signals or barrier semaphores. Data moves between devices by JAX's collectives and lax.ppermute only.
A program may use at most 64 MiB of HBM per device.

v0:
```python
import math

import jax
import jax.numpy as jnp
from jax import lax
from jax.sharding import PartitionSpec as P

NB = 1024
K = 4


def wave_tables(columns, samples):
    times = jnp.arange(samples, dtype=jnp.int32)
    phases = times[:, None] * columns[None, :] % samples
    angles = phases.astype(jnp.float32) * (2.0 * math.pi / samples)
    factor_scale = 1.0 / math.sqrt(samples)
    return jnp.concatenate(
        [jnp.cos(angles) * factor_scale, jnp.sin(angles) * factor_scale], axis=1
    ).astype(jnp.bfloat16)


def spectrum(flattened, wave_table, freq_here, base_here):
    width = wave_table.shape[1] // 2
    spectra = jnp.dot(flattened, wave_table, preferred_element_type=jnp.float32).reshape(
        freq_here, 2, base_here, 2, width
    )
    real_part = spectra[:, 0, :, 0] + spectra[:, 1, :, 1]
    imag_part = spectra[:, 1, :, 0] - spectra[:, 0, :, 1]
    return jnp.stack([real_part, imag_part], axis=1).astype(jnp.bfloat16)


def mask_round(coef, limits):
    rank_ids = jnp.arange(coef.shape[3], dtype=jnp.int32)
    retained = rank_ids[None, None, None, :] < limits[:, :, None, None]
    return jnp.where(retained, coef, 0.0).astype(jnp.bfloat16)


def local(vis_time, owner, counts, factors):
    n_freq = lax.axis_size("freq")
    myself = lax.axis_index("freq")
    freq_here, _, base_here, samples = vis_time.shape
    mode_count = owner.shape[0]
    capacity = factors.shape[0]
    slot_total = capacity * n_freq
    owners_of = owner[:, 0]
    owner_ids = jnp.arange(n_freq, dtype=jnp.int32)
    onehot = (owners_of[:, None] == owner_ids[None, :]).astype(jnp.int32)
    before = jnp.cumsum(onehot, axis=0) - onehot
    ranking = jnp.sum(before * onehot, axis=1)
    slot_of = owners_of * capacity + ranking
    mode_ids = jnp.arange(mode_count, dtype=jnp.int32)
    placing = slot_of[None, :] == jnp.arange(slot_total, dtype=jnp.int32)[:, None]
    placing_bf = placing.astype(jnp.bfloat16)
    flattened = vis_time.reshape(freq_here * 2 * base_here, samples)
    m_modes = spectrum(flattened, wave_tables(mode_ids, samples), freq_here, base_here)
    outgoing = jnp.einsum(
        "sm,fpbm->fspb", placing_bf, m_modes, preferred_element_type=jnp.float32
    ).astype(jnp.bfloat16)
    incoming = lax.all_to_all(outgoing, "freq", split_axis=1, concat_axis=0, tiled=True)
    mine = lax.dynamic_slice_in_dim(placing.astype(jnp.int32), myself * capacity, capacity, 0)
    limits = jnp.dot(mine, counts)
    fac_re = factors[:, :, 0]
    fac_im = factors[:, :, 1]
    vis_re = incoming[:, :, 0]
    vis_im = incoming[:, :, 1]
    coef_re = jnp.einsum(
        "cfkb,fcb->cfk", fac_re, vis_re, preferred_element_type=jnp.float32
    ) + jnp.einsum("cfkb,fcb->cfk", fac_im, vis_im, preferred_element_type=jnp.float32)
    coef_im = jnp.einsum(
        "cfkb,fcb->cfk", fac_re, vis_im, preferred_element_type=jnp.float32
    ) - jnp.einsum("cfkb,fcb->cfk", fac_im, vis_re, preferred_element_type=jnp.float32)
    partial_coef = jnp.stack([coef_re, coef_im], axis=2)
    summed = lax.psum(partial_coef, "bl")
    kept = mask_round(summed, limits)
    kept_re = kept[:, :, 0]
    kept_im = kept[:, :, 1]
    factor_scale = math.sqrt(NB / K)
    syn_re = (
        jnp.einsum("cfkb,cfk->fcb", fac_re, kept_re, preferred_element_type=jnp.float32)
        - jnp.einsum("cfkb,cfk->fcb", fac_im, kept_im, preferred_element_type=jnp.float32)
    ) * factor_scale
    syn_im = (
        jnp.einsum("cfkb,cfk->fcb", fac_re, kept_im, preferred_element_type=jnp.float32)
        + jnp.einsum("cfkb,cfk->fcb", fac_im, kept_re, preferred_element_type=jnp.float32)
    ) * factor_scale
    synthesis = jnp.stack([syn_re, syn_im], axis=2).astype(jnp.bfloat16)
    returned = lax.all_to_all(synthesis, "freq", split_axis=0, concat_axis=1, tiled=True)
    filtered = jnp.einsum("sm,fspb->fpbm", placing_bf, returned, preferred_element_type=jnp.float32)
    return filtered.astype(jnp.bfloat16)


def solution(mesh):
    placed = (P("freq", None, "bl", None), P(), P(), P("freq", None, None, None, "bl"))
    return jax.shard_map(
        local, mesh=mesh, in_specs=placed, out_specs=P("freq", None, "bl", None), check_vma=False
    )
```

profile of v0, /device:TPU:6, one launch (start us, length us, event | category | flops | bytes accessed | tf_op | source)
XLA Modules:
  0.0 161.8 jit_solution(7433060089402106239)
XLA Ops:
  0.0 13.9 %multiply_convert_fusion = (bf16[2048,384]{1,0:T(8,128)(2,1)}, bf16[2048,384]{1,0:T(8,128)(2,1)}) fusion(), kind=kLoop, calls=%fused_computation.10 | loop fusion | flops 14155776 | bytes 3145728 | tf_op jit(solution)/shard_map/convert.9
  14.0 0.1 copy.30
  14.1 0.2 fusion.45
  14.3 0.1 broadcast_add_fusion
  14.4 0.2 fusion.50
  14.7 4.9 %fusion.10 = f32[512,768]{0,1:T(8,128)} fusion(bf16[512,2048]{1,0:T(8,128)(2,1)S(1)} %bitcast.106, bf16[2048,384]{1,0:T(8,128)(2,1)} %get-tuple-element.15, bf16[2048,384]{1,0:T(8,128)(2,1)} %get-tuple-element.16), kind=kOutput, calls=%fused_computation.15 | convolution fusion | flops 1616904192 | bytes 6815744 | tf_op jit(solution)/shard_map/dot_general | solution.py:24
  19.5 3.1 %reshape.116 = f32[1,2,256,2,384]{2,1,4,3,0:T(2,128)} reshape(f32[512,768]{0,1:T(8,128)} %fusion.10) | data formatting | bytes 3145728 | tf_op jit(solution)/shard_map/reshape | solution.py:24
  22.6 4.1 %fusion.59 = (f32[1,1,256,1,384]{2,1,4,3,0:T(1,128)S(1)}, f32[1,1,256,1,384]{2,1,4,3,0:T(1,128)S(1)}, f32[1,1,256,1,384]{2,1,4,3,0:T(1,128)}, f32[1,1,256,1,384]{2,1,4,3,0:T(1,128)S(1)}) fusion(f32[1,2,256,2,384]{2,1,4,3,0:T(2,128)} %reshape.116), kind=kLoop, calls=%fused_computation.87 | loop fusion | bytes 3145728 | tf_op jit(solution)/shard_map/slice | solution.py:27
  26.7 1.9 %copy.55 = f32[1,1,256,1,384]{4,2,3,1,0:T(8,128)} copy(f32[1,1,256,1,384]{2,1,4,3,0:T(1,128)} %get-tuple-element.9) | data formatting | bytes 786432
  28.6 1.2 copy.56
  29.8 0.6 copy.57
  30.4 0.6 copy.58
  30.9 1.2 fusion.47
  32.1 0.0 copy-start.6
  32.2 0.5 fusion.13
  32.7 1.1 copy.36
  33.8 19.9 %all-to-all-start = ((bf16[1,512,2,256]{3,2,0,1:T(2,128)(2,1)}), bf16[1,512,2,256]{3,2,0,1:T(2,128)(2,1)S(1)}, u32[]{:S(2)}, u32[]{:S(2)}) async-start(bf16[1,512,2,256]{3,2,0,1:T(2,128)(2,1)} %copy.36), calls=%async_computation | async-start | bytes 1048576 | tf_op jit(solution)/shard_map/all_to_all | solution.py:59
  53.7 0.1 iota_compare_fusion
  53.8 0.2 fusion.54
  54.0 3.6 %slice_bitcast_fusion.1 = (bf16[4,128,4,256]{3,2,1,0:T(4,128)(2,1)}, bf16[4,128,4,256]{3,2,1,0:T(4,128)(2,1)}) fusion(bf16[4,128,2,4,256]{4,3,2,1,0:T(4,128)(2,1)} %param.7), kind=kLoop, calls=%fused_computation.21 | loop fusion | bytes 4194304 | tf_op jit(solution)/shard_map/squeeze | solution.py:62
  57.7 28.1 %all-to-all-done = bf16[1,512,2,256]{3,2,0,1:T(2,128)(2,1)S(1)} async-done(((bf16[1,512,2,256]{3,2,0,1:T(2,128)(2,1)}), bf16[1,512,2,256]{3,2,0,1:T(2,128)(2,1)S(1)}, u32[]{:S(2)}, u32[]{:S(2)}) %all-to-all-start) | async-done | bytes 524320 | tf_op jit(solution)/shard_map/all_to_all | solution.py:59
  85.8 0.7 fusion.60
  86.5 0.1 copy.92
  86.6 0.1 copy.91
  86.7 0.3 copy-done.2
  87.0 1.4 fusion.36
  88.5 0.7 fusion.30
  89.1 0.5 copy-done.1
  89.7 1.4 fusion.32
  91.1 1.4 fusion.34
  92.5 1.1 copy.42
  93.5 1.1 copy.44
  94.6 0.1 copy.45
  94.7 1.1 copy.46
  95.8 17.2 %psum.7 = bf16[4,128,2,4]{1,3,2,0:T(4,128)(2,1)S(1)} all-reduce(f32[4,128,2,4]{1,3,2,0:T(4,128)S(1)} %pad_maximum_fusion.1), channel_id=1, replica_groups=mesh['freq'=128,'bl'=4] {'bl'}, use_global_device_ids=true, to_apply=%region_3.4 | all-reduce | flops 4096 | bytes 24576 | tf_op jit(solution)/shard_map/psum | solution.py:73
  113.0 0.2 copy.50
  113.2 1.5 fusion.17
  114.7 1.5 fusion.19
  116.2 0.2 copy.47
  116.4 1.9 %fusion.21 = f32[128,4,1,256]{3,2,1,0:T(1,128)S(1)} fusion(bf16[4,128,4,1]{2,3,0,1:T(2,128)(2,1)S(1)} %copy.47, bf16[4,128,4,256]{3,2,1,0:T(4,128)(2,1)} %get-tuple-element.5), kind=kOutput, calls=%fused_computation.28 | convolution fusion | flops 1048576 | bytes 1576960 | tf_op jit(solution)/shard_map/cfkb,cfk->fcb/dot_general | solution.py:79
  118.4 0.7 fusion.15
  119.1 0.3 copy-done.5
  119.4 0.2 fusion.43
  119.6 0.2 fusion.44
  119.8 0.1 pad_maximum_fusion
  119.8 0.5 copy.39
  120.4 40.2 %all_to_all.21 = bf16[128,4,2,256]{3,2,1,0:T(2,128)(2,1)S(1)} all-to-all(bf16[128,4,2,256]{3,2,1,0:T(2,128)(2,1)S(1)} %copy.39), channel_id=1, replica_groups=mesh['freq'=128,'bl'=4] {'freq'}, dimensions={0} | all-to-all | bytes 1048576 | tf_op jit(solution)/shard_map/all_to_all | solution.py:87
  160.5 1.2 fusion.14
  (24 shorter events, 0.2 us)
Async XLA Ops:
  0.0 14.7 %copy-start = (bf16[1,2,256,2048]{3,2,1,0:T(8,128)(2,1)S(1)}, bf16[1,2,256,2048]{3,2,1,0:T(8,128)(2,1)}, u32[]{:S(2)}) copy-start(bf16[1,2,256,2048]{3,2,1,0:T(8,128)(2,1)} %param.4) | copy-start | bytes 6291460
  0.0 13.9 %copy-start.7 = (s32[384,1]{0,1:T(1,128)S(1)}, s32[384,1]{0,1:T(1,128)}, u32[]{:S(2)}) copy-start(s32[384,1]{0,1:T(1,128)} %param.5) | copy-start | bytes 4612
  32.1 21.7 %copy-start.6 = (s32[384,128]{1,0:T(8,128)S(1)}, s32[384,128]{1,0:T(8,128)}, u32[]{:S(2)}) copy-start(s32[384,128]{1,0:T(8,128)} %param.6) | copy-start | bytes 589828
  33.8 52.0 %all-to-all-start = ((bf16[1,512,2,256]{3,2,0,1:T(2,128)(2,1)}), bf16[1,512,2,256]{3,2,0,1:T(2,128)(2,1)S(1)}, u32[]{:S(2)}, u32[]{:S(2)}) async-start(bf16[1,512,2,256]{3,2,0,1:T(2,128)(2,1)} %copy.36), calls=%async_computation | async-start | bytes 1048576 | tf_op jit(solution)/shard_map/all_to_all | solution.py:59
  85.8 1.2 copy-start.2
  88.5 1.2 copy-start.1
  113.2 1.5 copy-start.3
  118.3 1.0 copy-start.5
  118.4 1.2 copy-start.4
where the time goes:
time: 164 us; the launch traced here: 162 us
  blocking collectives  57.3 us (35%)
  waiting for transfers between devices  28.1 us (17%)
  local copies, waits for them, and re-layouts  22.6 us (14%)
  starting transfers between devices  19.9 us (12%)
  matrix products  17.3 us (11%)
  other arithmetic  16.3 us (10%)
    all_to_all x1, blocking collectives, local(): lax.all_to_all(synthesis, 'freq', split_axis=0, concat_axis=1, tiled=True)  40.2 us
    all_to_all x1, waiting for transfers between devices, local(): lax.all_to_all(outgoing, 'freq', split_axis=1, concat_axis=0, tiled=True)  28.1 us
    all_to_all x1, starting transfers between devices, local(): lax.all_to_all(outgoing, 'freq', split_axis=1, concat_axis=0, tiled=True)  19.9 us
    psum x1, blocking collectives, local(): summed = lax.psum(partial_coef, 'bl')  17.2 us
    another operation x4, other arithmetic  14.2 us
    unnamed x20, local copies, waits for them, and re-layouts  5.46 us
    dot_general x1, matrix products, spectrum(): jnp.dot(flattened, wave_table, preferred_element_type=jnp.float32)  4.88 us
    slice x1, local copies, waits for them, and re-layouts, spectrum(): real_part = spectra[:, 0, :, 0] + spectra[:, 1, :, 1]  4.07 us
  transfers between devices with their start and end apart: 1, of which 1 were waited for; matrix products, arithmetic and copies ran while one was open for 2% of the time, Pallas kernels for 0%

commit v1 on v0

v1 whole, which is shorter than its diff:
```python
import math

import jax
import jax.numpy as jnp
import numpy as np
from jax import lax
from jax.experimental import pallas as pl
from jax.experimental.pallas import tpu as pltpu
from jax.sharding import PartitionSpec as P

NB = 1024
NT = 2048
K = 4
MM = 384
CAP = 4
STEPS = 4
F32 = jnp.float32
BF16 = jnp.bfloat16


def wave_rows():
    phases = np.outer(np.arange(MM), np.arange(NT)) % NT
    angles = phases * (2.0 * math.pi / NT)
    rows = np.concatenate([np.cos(angles), np.sin(angles)], axis=0) / math.sqrt(NT)
    return rows.astype(np.float32).astype(jnp.bfloat16)


def dft_kernel(owner_ref, vis_ref, wave_ref, out_ref, target_ref, acc_ref):
    step = pl.program_id(0)
    owners = out_ref.shape[0] // (2 * CAP)

    @pl.when(step == 0)
    def _():
        acc_ref[...] = jnp.zeros_like(acc_ref)
        hot = owner_ref[...] == lax.broadcasted_iota(jnp.int32, (owners, MM), 0)
        hot = jnp.where(hot, 1.0, 0.0)
        earlier = lax.broadcasted_iota(jnp.int32, (MM, MM), 0) < lax.broadcasted_iota(
            jnp.int32, (MM, MM), 1
        )
        earlier = jnp.where(earlier, 1.0, 0.0).astype(BF16)
        before = jnp.dot(hot.astype(BF16), earlier, preferred_element_type=F32)
        rank = jnp.sum(before * hot, axis=0, keepdims=True).astype(jnp.int32)
        target_ref[...] = owner_ref[...] * (2 * CAP) + rank

    acc_ref[...] += lax.dot_general(
        wave_ref[...], vis_ref[...], (((1,), (1,)), ((), ())), preferred_element_type=F32
    )

    @pl.when(step == pl.num_programs(0) - 1)
    def _():
        half = acc_ref.shape[1] // 2
        real = acc_ref[:MM, :half] + acc_ref[MM:, half:]
        imag = acc_ref[:MM, half:] - acc_ref[MM:, :half]
        modes = jnp.concatenate([real, imag], axis=0).astype(BF16)
        target = target_ref[...]
        target = jnp.concatenate([target, target + CAP], axis=1)
        rows = lax.broadcasted_iota(jnp.int32, (out_ref.shape[0], 2 * MM), 0)
        placing = jnp.where(rows == target, 1.0, 0.0).astype(BF16)
        out_ref[...] = jnp.dot(placing, modes, preferred_element_type=F32).astype(BF16)


def coef_kernel(vis_ref, fac_ref, out_ref):
    freqs, _, base = vis_ref.shape
    top = lax.broadcasted_iota(jnp.int32, (1, 2 * CAP, base), 1) < CAP
    lanes = lax.broadcasted_iota(jnp.int32, (2 * CAP, freqs), 1)
    block = 8

    def body(i, acc):
        first = pl.multiple_of(i * block, block)
        vis = vis_ref[pl.ds(first, block)].astype(F32)
        swapped = pltpu.roll(vis, CAP, 1)
        vis_re = jnp.where(top, vis, swapped)
        vis_im = jnp.where(top, swapped, vis)
        sums = []
        for pair in range(K // 2):
            fac_re = fac_ref[pl.ds(first, block), pl.ds(pair * 8, 8)].astype(F32)
            fac_im = fac_ref[pl.ds(first, block), pl.ds(16 + pair * 8, 8)].astype(F32)
            re = fac_re * vis_re + fac_im * vis_im
            im = fac_re * vis_im - fac_im * vis_re
            sums.append((jnp.sum(re, axis=2, keepdims=True), jnp.sum(im, axis=2, keepdims=True)))
        acc = list(acc)
        for j in range(block):
            here = lanes == first + j
            for ri in range(2):
                for pair in range(K // 2):
                    at = ri * 2 + pair
                    acc[at] = jnp.where(here, sums[pair][ri][j], acc[at])
        return tuple(acc)

    zero = jnp.zeros((2 * CAP, freqs), F32)
    acc = lax.fori_loop(0, freqs // block, body, (zero,) * 4)
    for at in range(4):
        for copy in range(out_ref.shape[0]):
            out_ref[copy, pl.ds(at * 8, 8), :] = acc[at]


def synth_kernel(part_ref, keep_ref, fac_ref, out_ref):
    freqs, _, base = out_ref.shape
    block = 8
    total = part_ref[0]
    for source in range(1, part_ref.shape[0]):
        total = total + part_ref[source]
    keep = keep_ref[...]
    keep = jnp.concatenate([keep, keep], axis=0)
    kept = jnp.where(keep > 0, total, 0.0).astype(BF16).astype(F32)
    kept = kept * math.sqrt(NB / K)
    top = lax.broadcasted_iota(jnp.int32, (2 * CAP, base), 0) < CAP

    def body(i, kept):
        first = pl.multiple_of(i * block, block)
        for j in range(block):
            re = jnp.zeros((2 * CAP, base), F32)
            im = jnp.zeros((2 * CAP, base), F32)
            for pair in range(K // 2):
                fac_re = fac_ref[first + j, pl.ds(pair * 8, 8)].astype(F32)
                fac_im = fac_ref[first + j, pl.ds(16 + pair * 8, 8)].astype(F32)
                kept_re = kept[pair * 8 : pair * 8 + 8, j : j + 1]
                kept_im = kept[16 + pair * 8 : 24 + pair * 8, j : j + 1]
                re = re + (fac_re * kept_re - fac_im * kept_im)
                im = im + (fac_re * kept_im + fac_im * kept_re)
            re = re + pltpu.roll(re, CAP, 0)
            im = im + pltpu.roll(im, CAP, 0)
            out_ref[first + j] = jnp.where(top, re, im).astype(BF16)
        return pltpu.roll(kept, freqs - block, 1)

    lax.fori_loop(0, freqs // block, body, kept)


def final_kernel(target_ref, slots_ref, out_ref):
    rows = lax.broadcasted_iota(jnp.int32, (slots_ref.shape[0], MM), 0)
    for part in range(2):
        placing = jnp.where(rows == target_ref[...] + part * CAP, 1.0, 0.0).astype(BF16)
        out_ref[part] = lax.dot_general(
            slots_ref[...], placing, (((0,), (0,)), ((), ())), preferred_element_type=F32
        ).astype(BF16)


def local(vis_time, owner, counts, factors):
    n_freq = lax.axis_size("freq")
    n_bl = lax.axis_size("bl")
    myself = lax.axis_index("freq")
    base = vis_time.shape[2]
    flat = vis_time.reshape(2 * base, NT)
    owner_row = owner.reshape(1, MM)
    width = 2 * CAP
    outgoing, target = pl.pallas_call(
        dft_kernel,
        grid=(STEPS,),
        in_specs=[
            pl.BlockSpec((1, MM), lambda i: (0, 0)),
            pl.BlockSpec((2 * base, NT // STEPS), lambda i: (0, i)),
            pl.BlockSpec((2 * MM, NT // STEPS), lambda i: (0, i)),
        ],
        out_specs=[
            pl.BlockSpec((n_freq * width, base), lambda i: (0, 0)),
            pl.BlockSpec((1, MM), lambda i: (0, 0)),
        ],
        out_shape=[
            jax.ShapeDtypeStruct((n_freq * width, base), BF16),
            jax.ShapeDtypeStruct((1, MM), jnp.int32),
        ],
        scratch_shapes=[pltpu.VMEM((2 * MM, 2 * base), F32)],
        compiler_params=pltpu.CompilerParams(vmem_limit_bytes=40 << 20),
        name="dft",
    )(owner_row, flat, jnp.asarray(wave_rows()))
    incoming = lax.all_to_all(
        outgoing.reshape(n_freq, width, base), "freq", split_axis=0, concat_axis=0, tiled=True
    )

    slot_rows = myself * width + jnp.arange(CAP, dtype=jnp.int32)
    mine = (target == slot_rows[:, None]).astype(BF16)
    limits = jnp.dot(mine, counts.astype(BF16), preferred_element_type=F32)
    keep = jnp.arange(K, dtype=F32)[:, None, None] < limits[None]
    keep = keep.astype(F32).reshape(K * CAP, n_freq)
    by_freq = jnp.transpose(factors, (1, 2, 3, 0, 4)).reshape(n_freq, 2 * K * CAP, base)

    partial = pl.pallas_call(
        coef_kernel,
        out_shape=jax.ShapeDtypeStruct((n_bl, 2 * K * CAP, n_freq), F32),
        compiler_params=pltpu.CompilerParams(vmem_limit_bytes=40 << 20),
        name="coef",
    )(incoming, by_freq)
    partials = lax.all_to_all(partial, "bl", split_axis=0, concat_axis=0, tiled=True)
    synthesis = pl.pallas_call(
        synth_kernel,
        out_shape=jax.ShapeDtypeStruct((n_freq, width, base), BF16),
        compiler_params=pltpu.CompilerParams(vmem_limit_bytes=40 << 20),
        name="synth",
    )(partials, keep, by_freq)
    returned = lax.all_to_all(synthesis, "freq", split_axis=0, concat_axis=0, tiled=True)
    filtered = pl.pallas_call(
        final_kernel,
        out_shape=jax.ShapeDtypeStruct((2, base, MM), BF16),
        compiler_params=pltpu.CompilerParams(vmem_limit_bytes=40 << 20),
        name="final",
    )(target, returned.reshape(n_freq * width, base))
    return filtered[None]


def solution(mesh):
    placed = (P("freq", None, "bl", None), P(), P(), P("freq", None, None, None, "bl"))
    return jax.shard_map(
        local, mesh=mesh, in_specs=placed, out_specs=P("freq", None, "bl", None), check_vma=False
    )
```

time: 164 us -> 119 us (0.73)
  matrix products: 17.3 us -> 0.18 us
  blocking collectives: 57.3 us -> 40.2 us
  other arithmetic: 16.3 us -> 0.1 us
  local copies, waits for them, and re-layouts: 22.6 us -> 10.9 us
  Pallas kernels: 0 us -> 10.7 us
  starting transfers between devices: 19.9 us -> 24.4 us
  waiting for transfers between devices: 28.1 us -> 30.7 us
    psum x1 -> x0, blocking collectives: 17.2 us -> none  [local(): summed = lax.psum(partial_coef, 'bl')]
    dot_general x12 -> x1, matrix products: 17.3 us -> 0.18 us  [local(): limits = jnp.dot(mine, counts.astype(BF16), preferred_element_type=F32)]
    another operation x10 -> x0, other arithmetic: 14.7 us -> none
    pallas_call x0 -> x4, Pallas kernels: none -> 10.7 us  [the longest x1 4.58 us: local(): pl.pallas_call(dft_kernel, grid=(STEPS,), in_specs=[pl.BlockSpec((1, MM),...]
    slice x4 -> x0, local copies, waits for them, and re-layouts: 4.96 us -> none  [the longest x1 4.07 us: spectrum(): real_part = spectra[:, 0, :, 0] + spectra[:, 1, :, 1]]
    all_to_all x1 -> x2, starting transfers between devices: 19.9 us -> 24.4 us  [the longest x1 19.9 us: local(): lax.all_to_all(outgoing.reshape(n_freq, width, base), 'freq', split_axis=...]
    transpose x0 -> x1, local copies, waits for them, and re-layouts: none -> 4.05 us  [local(): jnp.transpose(factors, (1, 2, 3, 0, 4)).reshape(n_freq, 2 * K * CAP, base)]
    squeeze x4 -> x0, local copies, waits for them, and re-layouts: 4 us -> none  [the longest x1 3.61 us: local(): fac_re = factors[:, :, 0]]
  transfers between devices with their start and end apart: 1 -> 2, of which waited for: 1 -> 2; matrix products, arithmetic and copies ran while one was open for 2% -> 6% of each run, Pallas kernels for 0% -> 0%
where the time goes in v1:
time: 119 us; the launch traced here: 117 us
  blocking collectives  40.2 us (34%)
  waiting for transfers between devices  30.7 us (26%)
  starting transfers between devices  24.4 us (21%)
  local copies, waits for them, and re-layouts  10.9 us (9%)
  Pallas kernels  10.7 us (9%)
    all_to_all x1, blocking collectives, local(): lax.all_to_all(synthesis, 'freq', split_axis=0, concat_axis=0, tiled=True)  40.2 us
    all_to_all x1, waiting for transfers between devices, local(): lax.all_to_all(outgoing.reshape(n_freq, width, base), 'freq', split_axis=...  25.1 us
    all_to_all x1, starting transfers between devices, local(): lax.all_to_all(outgoing.reshape(n_freq, width, base), 'freq', split_axis=...  19.9 us
    all_to_all x1, waiting for transfers between devices, local(): lax.all_to_all(partial, 'bl', split_axis=0, concat_axis=0, tiled=True)  5.55 us
    pallas_call x1, Pallas kernels, local(): pl.pallas_call(dft_kernel, grid=(STEPS,), in_specs=[pl.BlockSpec((1, MM),...  4.58 us
    all_to_all x1, starting transfers between devices, local(): lax.all_to_all(partial, 'bl', split_axis=0, concat_axis=0, tiled=True)  4.47 us
    unnamed x10, local copies, waits for them, and re-layouts  4.17 us
    transpose x1, local copies, waits for them, and re-layouts, local(): jnp.transpose(factors, (1, 2, 3, 0, 4)).reshape(n_freq, 2 * K * CAP, base)  4.05 us
  transfers between devices with their start and end apart: 2, of which 2 were waited for; matrix products, arithmetic and copies ran while one was open for 6% of the time, Pallas kernels for 0%

profile of v1, /device:TPU:6, one launch (start us, length us, event | category | flops | bytes accessed | tf_op | source)
XLA Modules:
  0.0 117.2 jit_solution(11257808786145829275)
XLA Ops:
  0.0 0.0 copy-start
  0.0 1.9 %copy-done = bf16[768,2048]{1,0:T(8,128)(2,1)S(1)} copy-done((bf16[768,2048]{1,0:T(8,128)(2,1)S(1)}, bf16[768,2048]{1,0:T(8,128)(2,1)}, u32[]{:S(2)}) %copy-start) | copy-done | bytes 3145752
  1.9 0.0 copy-start.1
  1.9 1.6 %copy-done.1 = bf16[1,2,256,2048]{3,2,1,0:T(8,128)(2,1)S(1)} copy-done((bf16[1,2,256,2048]{3,2,1,0:T(8,128)(2,1)S(1)}, bf16[1,2,256,2048]{3,2,1,0:T(8,128)(2,1)}, u32[]{:S(2)}) %copy-start.1) | copy-done | bytes 2097176
  3.5 0.0 copy-start.2
  3.5 0.7 copy-done.2
  4.2 0.0 copy-start.3
  4.2 4.6 %dft.1 = (bf16[1024,256]{1,0:T(8,128)(2,1)}, s32[1,384]{1,0:T(1,128)S(1)}) custom-call(s32[1,384]{1,0:T(1,128)S(1)} %bitcast.9, bf16[512,2048]{1,0:T(8,128)(2,1)S(1)} %bitcast.7, bf16[768,2048]{1,0:T(8,128)(2,1)S(1)} %copy-done), custom_call_target="tpu_custom_call" | custom-call | tf_op jit(solution)/shard_map/dft/pallas_call | solution.py:146
  8.7 19.9 %all-to-all-start = ((bf16[128,8,256]{2,1,0:T(8,128)(2,1)}), bf16[128,8,256]{2,1,0:T(8,128)(2,1)S(1)}, u32[]{:S(2)}, u32[]{:S(2)}) async-start(bf16[128,8,256]{2,1,0:T(8,128)(2,1)} %bitcast.2), calls=%async_computation | async-start | bytes 1048576 | tf_op jit(solution)/shard_map/all_to_all | solution.py:166
  28.7 0.0 copy-done.3
  28.7 4.0 %copy.6 = bf16[128,2,4,4,256]{4,3,2,1,0:T(4,128)(2,1)} copy(bf16[128,2,4,4,256]{4,2,1,0,3:T(4,128)(2,1)S(1)} %bitcast.10) | data formatting | bytes 4194304 | tf_op jit(solution)/shard_map/transpose | solution.py:175
  32.7 0.0 copy-start.4
  32.7 2.6 %reshape.26.fac_ref = bf16[128,32,256]{2,1,0:T(8,128)(2,1)S(1)} reshape(bf16[128,2,4,4,256]{4,3,2,1,0:T(4,128)(2,1)} %copy.6) | data formatting | bytes 4194304 | tf_op jit(solution)/shard_map/reshape | solution.py:175
  35.3 0.1 lt.21
  35.5 0.0 copy-done.4
  35.5 0.2 fusion
  35.6 25.1 %all-to-all-done.vis_ref = bf16[128,8,256]{2,1,0:T(8,128)(2,1)S(1)} async-done(((bf16[128,8,256]{2,1,0:T(8,128)(2,1)}), bf16[128,8,256]{2,1,0:T(8,128)(2,1)S(1)}, u32[]{:S(2)}, u32[]{:S(2)}) %all-to-all-start) | async-done | bytes 524320 | tf_op jit(solution)/shard_map/all_to_all | solution.py:166
  60.8 2.6 %coef.1 = f32[4,32,128]{2,1,0:T(8,128)} custom-call(bf16[128,8,256]{2,1,0:T(8,128)(2,1)S(1)} %all-to-all-done.vis_ref, bf16[128,32,256]{2,1,0:T(8,128)(2,1)S(1)} %reshape.26.fac_ref), custom_call_target="tpu_custom_call" | custom-call | tf_op jit(solution)/shard_map/coef/pallas_call | solution.py:177
  63.4 4.5 %all-to-all-start.1 = ((f32[4,32,128]{2,1,0:T(8,128)}), f32[4,32,128]{2,1,0:T(8,128)S(1)}, u32[]{:S(2)}, u32[]{:S(2)}) async-start(f32[4,32,128]{2,1,0:T(8,128)} %coef.1), calls=%async_computation.1 | async-start | bytes 131072 | tf_op jit(solution)/shard_map/all_to_all | solution.py:183
  67.9 0.1 compare_convert_fusion.keep_ref
  68.0 5.5 %all-to-all-done.1.part_ref = f32[4,32,128]{2,1,0:T(8,128)S(1)} async-done(((f32[4,32,128]{2,1,0:T(8,128)}), f32[4,32,128]{2,1,0:T(8,128)S(1)}, u32[]{:S(2)}, u32[]{:S(2)}) %all-to-all-start.1) | async-done | bytes 65568 | tf_op jit(solution)/shard_map/all_to_all | solution.py:183
  73.5 2.0 %synth.1 = bf16[128,8,256]{2,1,0:T(8,128)(2,1)S(1)} custom-call(f32[4,32,128]{2,1,0:T(8,128)S(1)} %all-to-all-done.1.part_ref, f32[16,128]{1,0:T(8,128)S(1)} %compare_convert_fusion.keep_ref, bf16[128,32,256]{2,1,0:T(8,128)(2,1)S(1)} %reshape.26.fac_ref), custom_call_target="tpu_custom_call" | custom-call | tf_op jit(solution)/shard_map/synth/pallas_call | solution.py:184
  75.5 40.2 %all_to_all.15 = bf16[128,8,256]{2,1,0:T(8,128)(2,1)S(1)} all-to-all(bf16[128,8,256]{2,1,0:T(8,128)(2,1)S(1)} %synth.1), channel_id=1, replica_groups=mesh['freq'=128,'bl'=4] {'freq'}, dimensions={0} | all-to-all | bytes 1048576 | tf_op jit(solution)/shard_map/all_to_all | solution.py:190
  115.6 1.5 %final.1 = bf16[2,256,384]{2,1,0:T(8,128)(2,1)} custom-call(s32[1,384]{1,0:T(1,128)S(1)} %get-tuple-element.7.target_ref, bf16[1024,256]{1,0:T(8,128)(2,1)S(1)} %bitcast.8), custom_call_target="tpu_custom_call" | custom-call | tf_op jit(solution)/shard_map/final/pallas_call | solution.py:191
  (4 shorter events, 0.0 us)
Async XLA Ops:
  0.0 1.9 %copy-start = (bf16[768,2048]{1,0:T(8,128)(2,1)S(1)}, bf16[768,2048]{1,0:T(8,128)(2,1)}, u32[]{:S(2)}) copy-start(bf16[768,2048]{1,0:T(8,128)(2,1)} %constant.10.clone.wave_ref) | copy-start | bytes 9437188
  1.9 1.6 %copy-start.1 = (bf16[1,2,256,2048]{3,2,1,0:T(8,128)(2,1)S(1)}, bf16[1,2,256,2048]{3,2,1,0:T(8,128)(2,1)}, u32[]{:S(2)}) copy-start(bf16[1,2,256,2048]{3,2,1,0:T(8,128)(2,1)} %param.5) | copy-start | bytes 6291460
  3.5 0.7 copy-start.2
  4.2 24.5 %copy-start.3 = (bf16[4,128,2,4,256]{4,3,2,1,0:T(4,128)(2,1)S(1)}, bf16[4,128,2,4,256]{4,3,2,1,0:T(4,128)(2,1)}, u32[]{:S(2)}) copy-start(bf16[4,128,2,4,256]{4,3,2,1,0:T(4,128)(2,1)} %param.8) | copy-start | bytes 6291460
  8.7 52.0 %all-to-all-start = ((bf16[128,8,256]{2,1,0:T(8,128)(2,1)}), bf16[128,8,256]{2,1,0:T(8,128)(2,1)S(1)}, u32[]{:S(2)}, u32[]{:S(2)}) async-start(bf16[128,8,256]{2,1,0:T(8,128)(2,1)} %bitcast.2), calls=%async_computation | async-start | bytes 1048576 | tf_op jit(solution)/shard_map/all_to_all | solution.py:166
  32.7 2.7 %copy-start.4 = (s32[384,128]{1,0:T(8,128)S(1)}, s32[384,128]{1,0:T(8,128)}, u32[]{:S(2)}) copy-start(s32[384,128]{1,0:T(8,128)} %param.7) | copy-start | bytes 589828
  63.4 10.1 %all-to-all-start.1 = ((f32[4,32,128]{2,1,0:T(8,128)}), f32[4,32,128]{2,1,0:T(8,128)S(1)}, u32[]{:S(2)}, u32[]{:S(2)}) async-start(f32[4,32,128]{2,1,0:T(8,128)} %coef.1), calls=%async_computation.1 | async-start | bytes 131072 | tf_op jit(solution)/shard_map/all_to_all | solution.py:183

commit v2 on v1

--- a/solution.py
+++ b/solution.py
@@ -13,57 +13,81 @@
 K = 4
 MM = 384
 CAP = 4
-STEPS = 4
+CHUNK = NT // 4
+BLOCK = 32
 F32 = jnp.float32
 BF16 = jnp.bfloat16
 
 
-def wave_rows():
-    phases = np.outer(np.arange(MM), np.arange(NT)) % NT
+def wave_half():
+    phases = np.outer(np.arange(NT // 2), np.arange(MM)) % NT
     angles = phases * (2.0 * math.pi / NT)
-    rows = np.concatenate([np.cos(angles), np.sin(angles)], axis=0) / math.sqrt(NT)
+    rows = np.concatenate([np.cos(angles), np.sin(angles)], axis=1) / math.sqrt(NT)
     return rows.astype(np.float32).astype(jnp.bfloat16)
 
 
-def dft_kernel(owner_ref, vis_ref, wave_ref, out_ref, target_ref, acc_ref):
-    step = pl.program_id(0)
+def dft_kernel(owner_hbm, vis_hbm, wave_hbm, out_ref, target_ref, owner_ref, vis_ref, wave_ref, sems):
     owners = out_ref.shape[0] // (2 * CAP)
-
-    @pl.when(step == 0)
-    def _():
-        acc_ref[...] = jnp.zeros_like(acc_ref)
-        hot = owner_ref[...] == lax.broadcasted_iota(jnp.int32, (owners, MM), 0)
-        hot = jnp.where(hot, 1.0, 0.0)
-        earlier = lax.broadcasted_iota(jnp.int32, (MM, MM), 0) < lax.broadcasted_iota(
-            jnp.int32, (MM, MM), 1
+    owner_copy = pltpu.make_async_copy(owner_hbm, owner_ref, sems.at[0])
+    owner_copy.start()
+    wave_copies, vis_copies = [], {}
+    for part in range(2):
+        wave_copies.append(
+            pltpu.make_async_copy(
+                wave_hbm.at[pl.ds(part * CHUNK, CHUNK)], wave_ref.at[part], sems.at[1 + part]
+            )
         )
-        earlier = jnp.where(earlier, 1.0, 0.0).astype(BF16)
-        before = jnp.dot(hot.astype(BF16), earlier, preferred_element_type=F32)
-        rank = jnp.sum(before * hot, axis=0, keepdims=True).astype(jnp.int32)
-        target_ref[...] = owner_ref[...] * (2 * CAP) + rank
-
-    acc_ref[...] += lax.dot_general(
-        wave_ref[...], vis_ref[...], (((1,), (1,)), ((), ())), preferred_element_type=F32
+        wave_copies[-1].start()
+        for chunk in (part, part + 2):
+            vis_copies[chunk] = pltpu.make_async_copy(
+                vis_hbm.at[:, pl.ds(chunk * CHUNK, CHUNK)], vis_ref.at[chunk], sems.at[3 + chunk]
+            )
+            vis_copies[chunk].start()
+    owner_copy.wait()
+    owner = owner_ref[...]
+    hot = owner == lax.broadcasted_iota(jnp.int32, (owners, MM), 0)
+    hot = jnp.where(hot, 1.0, 0.0)
+    earlier = lax.broadcasted_iota(jnp.int32, (MM, MM), 0) < lax.broadcasted_iota(
+        jnp.int32, (MM, MM), 1
     )
-
-    @pl.when(step == pl.num_programs(0) - 1)
-    def _():
-        half = acc_ref.shape[1] // 2
-        real = acc_ref[:MM, :half] + acc_ref[MM:, half:]
-        imag = acc_ref[:MM, half:] - acc_ref[MM:, :half]
-        modes = jnp.concatenate([real, imag], axis=0).astype(BF16)
-        target = target_ref[...]
-        target = jnp.concatenate([target, target + CAP], axis=1)
-        rows = lax.broadcasted_iota(jnp.int32, (out_ref.shape[0], 2 * MM), 0)
-        placing = jnp.where(rows == target, 1.0, 0.0).astype(BF16)
-        out_ref[...] = jnp.dot(placing, modes, preferred_element_type=F32).astype(BF16)
-
-
-def coef_kernel(vis_ref, fac_ref, out_ref):
+    earlier = jnp.where(earlier, 1.0, 0.0).astype(BF16)
+    before = jnp.dot(hot.astype(BF16), earlier, preferred_element_type=F32)
+    rank = jnp.sum(before * hot, axis=0, keepdims=True).astype(jnp.int32)
+    target = owner * (2 * CAP) + rank
+    target_ref[...] = target
+    target = jnp.concatenate([target, target + CAP], axis=1)
+    rows = lax.broadcasted_iota(jnp.int32, (out_ref.shape[0], 2 * MM), 0)
+    placing = jnp.where(rows == target, 1.0, 0.0).astype(BF16)
+
+    sign = 1 - 2 * (lax.broadcasted_iota(jnp.int32, (1, 2 * MM), 1) % 2)
+    sign = sign.astype(F32)
+    spectra = None
+    for part in range(2):
+        wave_copies[part].wait()
+        for half in range(2):
+            chunk = part + 2 * half
+            vis_copies[chunk].wait()
+            product = jnp.dot(vis_ref[chunk], wave_ref[part], preferred_element_type=F32)
+            if half == 1:
+                product = product * sign
+            spectra = product if spectra is None else spectra + product
+    base = spectra.shape[0] // 2
+    real = spectra[:base, :MM] + spectra[base:, MM:]
+    imag = spectra[base:, :MM] - spectra[:base, MM:]
+    modes = jnp.concatenate([real, imag], axis=1).astype(BF16)
+    out_ref[...] = lax.dot_general(
+        placing, modes, (((1,), (1,)), ((), ())), preferred_element_type=F32
+    ).astype(BF16)
+
+
+def coef_kernel(vis_ref, fac_ref, limit_ref, out_ref, keep_ref):
     freqs, _, base = vis_ref.shape
     top = lax.broadcasted_iota(jnp.int32, (1, 2 * CAP, base), 1) < CAP
     lanes = lax.broadcasted_iota(jnp.int32, (2 * CAP, freqs), 1)
-    block = 8
+    block = BLOCK
+    ranks = lax.broadcasted_iota(jnp.int32, (2 * K * CAP, freqs), 0) // CAP % K
+    limits = jnp.concatenate([limit_ref[...]] * (2 * K), axis=0)
+    keep_ref[...] = jnp.where(ranks.astype(F32) < limits, 1.0, 0.0)
 
     def body(i, acc):
         first = pl.multiple_of(i * block, block)
@@ -96,13 +120,11 @@
 
 def synth_kernel(part_ref, keep_ref, fac_ref, out_ref):
     freqs, _, base = out_ref.shape
-    block = 8
+    block = BLOCK
     total = part_ref[0]
     for source in range(1, part_ref.shape[0]):
         total = total + part_ref[source]
-    keep = keep_ref[...]
-    keep = jnp.concatenate([keep, keep], axis=0)
-    kept = jnp.where(keep > 0, total, 0.0).astype(BF16).astype(F32)
+    kept = jnp.where(keep_ref[...] > 0, total, 0.0).astype(BF16).astype(F32)
     kept = kept * math.sqrt(NB / K)
     top = lax.broadcasted_iota(jnp.int32, (2 * CAP, base), 0) < CAP
 
@@ -143,26 +165,24 @@
     flat = vis_time.reshape(2 * base, NT)
     owner_row = owner.reshape(1, MM)
     width = 2 * CAP
+    hbm = pl.BlockSpec(memory_space=pltpu.HBM)
+    wave = jnp.asarray(wave_half())
     outgoing, target = pl.pallas_call(
         dft_kernel,
-        grid=(STEPS,),
-        in_specs=[
-            pl.BlockSpec((1, MM), lambda i: (0, 0)),
-            pl.BlockSpec((2 * base, NT // STEPS), lambda i: (0, i)),
-            pl.BlockSpec((2 * MM, NT // STEPS), lambda i: (0, i)),
-        ],
-        out_specs=[
-            pl.BlockSpec((n_freq * width, base), lambda i: (0, 0)),
-            pl.BlockSpec((1, MM), lambda i: (0, 0)),
-        ],
+        in_specs=[hbm, hbm, hbm],
         out_shape=[
             jax.ShapeDtypeStruct((n_freq * width, base), BF16),
             jax.ShapeDtypeStruct((1, MM), jnp.int32),
         ],
-        scratch_shapes=[pltpu.VMEM((2 * MM, 2 * base), F32)],
+        scratch_shapes=[
+            pltpu.VMEM((1, MM), jnp.int32),
+            pltpu.VMEM((4, 2 * base, CHUNK), BF16),
+            pltpu.VMEM((2, CHUNK, 2 * MM), BF16),
+            pltpu.SemaphoreType.DMA((7,)),
+        ],
         compiler_params=pltpu.CompilerParams(vmem_limit_bytes=40 << 20),
         name="dft",
-    )(owner_row, flat, jnp.asarray(wave_rows()))
+    )(*(pltpu.with_memory_space_constraint(a, pltpu.HBM) for a in (owner_row, flat, wave)))
     incoming = lax.all_to_all(
         outgoing.reshape(n_freq, width, base), "freq", split_axis=0, concat_axis=0, tiled=True
     )
@@ -170,16 +190,17 @@
     slot_rows = myself * width + jnp.arange(CAP, dtype=jnp.int32)
     mine = (target == slot_rows[:, None]).astype(BF16)
     limits = jnp.dot(mine, counts.astype(BF16), preferred_element_type=F32)
-    keep = jnp.arange(K, dtype=F32)[:, None, None] < limits[None]
-    keep = keep.astype(F32).reshape(K * CAP, n_freq)
     by_freq = jnp.transpose(factors, (1, 2, 3, 0, 4)).reshape(n_freq, 2 * K * CAP, base)
 
-    partial = pl.pallas_call(
+    partial, keep = pl.pallas_call(
         coef_kernel,
-        out_shape=jax.ShapeDtypeStruct((n_bl, 2 * K * CAP, n_freq), F32),
+        out_shape=[
+            jax.ShapeDtypeStruct((n_bl, 2 * K * CAP, n_freq), F32),
+            jax.ShapeDtypeStruct((2 * K * CAP, n_freq), F32),
+        ],
         compiler_params=pltpu.CompilerParams(vmem_limit_bytes=40 << 20),
         name="coef",
-    )(incoming, by_freq)
+    )(incoming, by_freq, limits)
     partials = lax.all_to_all(partial, "bl", split_axis=0, concat_axis=0, tiled=True)
     synthesis = pl.pallas_call(
         synth_kernel,

time: 119 us -> 113 us (0.950)
  blocking collectives: 40.2 us -> 50.1 us
  waiting for transfers between devices: 30.7 us -> 25.2 us
  starting transfers between devices: 24.4 us -> 19.9 us
  local copies, waits for them, and re-layouts: 10.9 us -> 6.62 us
  Pallas kernels: 10.7 us -> 9.25 us
    all_to_all x0 -> x1, blocking collectives: none -> 9.89 us  [local(): lax.all_to_all(partial, 'bl', split_axis=0, concat_axis=0, tiled=True)]
    all_to_all x1 -> x0, waiting for transfers between devices: 5.55 us -> none  [local(): lax.all_to_all(partial, 'bl', split_axis=0, concat_axis=0, tiled=True)]
    all_to_all x1 -> x0, starting transfers between devices: 4.47 us -> none  [local(): lax.all_to_all(partial, 'bl', split_axis=0, concat_axis=0, tiled=True)]
    unnamed x10 -> x4, local copies, waits for them, and re-layouts: 4.17 us -> 0.01 us
  transfers between devices with their start and end apart: 2 -> 1, of which waited for: 2 -> 1; matrix products, arithmetic and copies ran while one was open for 6% -> 6% of each run, Pallas kernels for 0% -> 0%
where the time goes in v2:
time: 113 us; the launch traced here: 111 us
  blocking collectives  50.1 us (44%)
  waiting for transfers between devices  25.2 us (22%)
  starting transfers between devices  19.9 us (18%)
  Pallas kernels  9.25 us (8%)
  local copies, waits for them, and re-layouts  6.62 us (6%)
    all_to_all x1, blocking collectives, local(): lax.all_to_all(synthesis, 'freq', split_axis=0, concat_axis=0, tiled=True)  40.2 us
    all_to_all x1, waiting for transfers between devices, local(): lax.all_to_all(outgoing.reshape(n_freq, width, base), 'freq', split_axis=...  25.2 us
    all_to_all x1, starting transfers between devices, local(): lax.all_to_all(outgoing.reshape(n_freq, width, base), 'freq', split_axis=...  19.9 us
    all_to_all x1, blocking collectives, local(): lax.all_to_all(partial, 'bl', split_axis=0, concat_axis=0, tiled=True)  9.89 us
    pallas_call x1, Pallas kernels, local(): pl.pallas_call(dft_kernel, in_specs=[hbm, hbm, hbm], out_shape=[jax.Shape...  5.26 us
    transpose x1, local copies, waits for them, and re-layouts, local(): jnp.transpose(factors, (1, 2, 3, 0, 4)).reshape(n_freq, 2 * K * CAP, base)  4.03 us
    reshape x1, local copies, waits for them, and re-layouts, local(): jnp.transpose(factors, (1, 2, 3, 0, 4)).reshape(n_freq, 2 * K * CAP, base)  2.58 us
  transfers between devices with their start and end apart: 1, of which 1 were waited for; matrix products, arithmetic and copies ran while one was open for 6% of the time, Pallas kernels for 0%

profile of v2, /device:TPU:6, one launch (start us, length us, event | category | flops | bytes accessed | tf_op | source)
XLA Modules:
  0.0 111.4 jit_solution(11408634739989350215)
XLA Ops:
  0.0 0.0 copy-start
  0.0 5.3 %dft.1 = (bf16[1024,256]{1,0:T(8,128)(2,1)}, s32[1,384]{1,0:T(1,128)S(1)}) custom-call(s32[1,384]{1,0:T(1,128)} %bitcast.9, bf16[512,2048]{1,0:T(8,128)(2,1)} %bitcast.7, bf16[1024,768]{1,0:T(8,128)(2,1)} %constant.10.clone.wave_hbm), custom_call_target="tpu_custom_call" | custom-call | tf_op jit(solution)/shard_map/dft/pallas_call | solution.py:170
  5.3 19.9 %all-to-all-start = ((bf16[128,8,256]{2,1,0:T(8,128)(2,1)}), bf16[128,8,256]{2,1,0:T(8,128)(2,1)S(1)}, u32[]{:S(2)}, u32[]{:S(2)}) async-start(bf16[128,8,256]{2,1,0:T(8,128)(2,1)} %bitcast.2), calls=%async_computation | async-start | bytes 1048576 | tf_op jit(solution)/shard_map/all_to_all | solution.py:186
  25.2 0.0 copy-done
  25.2 4.0 %copy.6 = bf16[128,2,4,4,256]{4,3,2,1,0:T(4,128)(2,1)} copy(bf16[128,2,4,4,256]{4,2,1,0,3:T(4,128)(2,1)S(1)} %bitcast.8) | data formatting | bytes 4194304 | tf_op jit(solution)/shard_map/transpose | solution.py:193
  29.2 0.0 copy-start.1
  29.2 2.6 %reshape.22.fac_ref = bf16[128,32,256]{2,1,0:T(8,128)(2,1)S(1)} reshape(bf16[128,2,4,4,256]{4,3,2,1,0:T(4,128)(2,1)} %copy.6) | data formatting | bytes 4194304 | tf_op jit(solution)/shard_map/reshape | solution.py:193
  31.9 0.0 copy-done.1
  31.9 0.2 fusion.limit_ref
  32.1 25.2 %all-to-all-done.vis_ref = bf16[128,8,256]{2,1,0:T(8,128)(2,1)S(1)} async-done(((bf16[128,8,256]{2,1,0:T(8,128)(2,1)}), bf16[128,8,256]{2,1,0:T(8,128)(2,1)S(1)}, u32[]{:S(2)}, u32[]{:S(2)}) %all-to-all-start) | async-done | bytes 524320 | tf_op jit(solution)/shard_map/all_to_all | solution.py:186
  57.3 1.3 %coef.1 = (f32[4,32,128]{2,1,0:T(8,128)S(1)}, f32[32,128]{1,0:T(8,128)S(1)}) custom-call(bf16[128,8,256]{2,1,0:T(8,128)(2,1)S(1)} %all-to-all-done.vis_ref, bf16[128,32,256]{2,1,0:T(8,128)(2,1)S(1)} %reshape.22.fac_ref, f32[4,128]{1,0:T(4,128)S(1)} %fusion.limit_ref), custom_call_target="tpu_custom_call" | custom-call | tf_op jit(solution)/shard_map/coef/pallas_call | solution.py:195
  58.6 9.9 %all_to_all.15.part_ref = f32[4,32,128]{2,1,0:T(8,128)S(1)} all-to-all(f32[4,32,128]{2,1,0:T(8,128)S(1)} %get-tuple-element.11), channel_id=1, replica_groups=mesh['freq'=128,'bl'=4] {'bl'}, dimensions={0} | all-to-all | bytes 131072 | tf_op jit(solution)/shard_map/all_to_all | solution.py:204
  68.5 1.2 %synth.1 = bf16[128,8,256]{2,1,0:T(8,128)(2,1)S(1)} custom-call(f32[4,32,128]{2,1,0:T(8,128)S(1)} %all_to_all.15.part_ref, f32[32,128]{1,0:T(8,128)S(1)} %get-tuple-element.12.keep_ref, bf16[128,32,256]{2,1,0:T(8,128)(2,1)S(1)} %reshape.22.fac_ref), custom_call_target="tpu_custom_call" | custom-call | tf_op jit(solution)/shard_map/synth/pallas_call | solution.py:205
  69.7 40.2 %all_to_all.16 = bf16[128,8,256]{2,1,0:T(8,128)(2,1)S(1)} all-to-all(bf16[128,8,256]{2,1,0:T(8,128)(2,1)S(1)} %synth.1), channel_id=1, replica_groups=mesh['freq'=128,'bl'=4] {'freq'}, dimensions={0} | all-to-all | bytes 1048576 | tf_op jit(solution)/shard_map/all_to_all | solution.py:211
  109.8 1.5 %final.1 = bf16[2,256,384]{2,1,0:T(8,128)(2,1)} custom-call(s32[1,384]{1,0:T(1,128)S(1)} %get-tuple-element.9.target_ref, bf16[1024,256]{1,0:T(8,128)(2,1)S(1)} %bitcast.6), custom_call_target="tpu_custom_call" | custom-call | tf_op jit(solution)/shard_map/final/pallas_call | solution.py:212
  (2 shorter events, 0.0 us)
Async XLA Ops:
  0.0 25.2 %copy-start = (bf16[4,128,2,4,256]{4,3,2,1,0:T(4,128)(2,1)S(1)}, bf16[4,128,2,4,256]{4,3,2,1,0:T(4,128)(2,1)}, u32[]{:S(2)}) copy-start(bf16[4,128,2,4,256]{4,3,2,1,0:T(4,128)(2,1)} %param.8) | copy-start | bytes 6291460
  5.3 52.0 %all-to-all-start = ((bf16[128,8,256]{2,1,0:T(8,128)(2,1)}), bf16[128,8,256]{2,1,0:T(8,128)(2,1)S(1)}, u32[]{:S(2)}, u32[]{:S(2)}) async-start(bf16[128,8,256]{2,1,0:T(8,128)(2,1)} %bitcast.2), calls=%async_computation | async-start | bytes 1048576 | tf_op jit(solution)/shard_map/all_to_all | solution.py:186
  29.2 2.6 %copy-start.1 = (s32[384,128]{1,0:T(8,128)S(1)}, s32[384,128]{1,0:T(8,128)}, u32[]{:S(2)}) copy-start(s32[384,128]{1,0:T(8,128)} %param.7) | copy-start | bytes 589828

commit v3 on v2

--- a/solution.py
+++ b/solution.py
@@ -80,47 +80,44 @@
     ).astype(BF16)
 
 
-def coef_kernel(vis_ref, fac_ref, limit_ref, out_ref, keep_ref):
-    freqs, _, base = vis_ref.shape
+def coef_kernel(core_ref, vis_ref, own_ref, other_ref, limit_ref, out_ref, keep_ref):
+    core = core_ref[0]
+    pairs, _, base = vis_ref.shape
     top = lax.broadcasted_iota(jnp.int32, (1, 2 * CAP, base), 1) < CAP
-    lanes = lax.broadcasted_iota(jnp.int32, (2 * CAP, freqs), 1)
-    block = BLOCK
-    ranks = lax.broadcasted_iota(jnp.int32, (2 * K * CAP, freqs), 0) // CAP % K
+    lanes = lax.broadcasted_iota(jnp.int32, (2 * CAP, pairs), 1)
+    ranks = lax.broadcasted_iota(jnp.int32, (2 * K * CAP, pairs), 0) // CAP % K
     limits = jnp.concatenate([limit_ref[...]] * (2 * K), axis=0)
     keep_ref[...] = jnp.where(ranks.astype(F32) < limits, 1.0, 0.0)
 
     def body(i, acc):
-        first = pl.multiple_of(i * block, block)
-        vis = vis_ref[pl.ds(first, block)].astype(F32)
-        swapped = pltpu.roll(vis, CAP, 1)
-        vis_re = jnp.where(top, vis, swapped)
-        vis_im = jnp.where(top, swapped, vis)
-        sums = []
-        for pair in range(K // 2):
-            fac_re = fac_ref[pl.ds(first, block), pl.ds(pair * 8, 8)].astype(F32)
-            fac_im = fac_ref[pl.ds(first, block), pl.ds(16 + pair * 8, 8)].astype(F32)
-            re = fac_re * vis_re + fac_im * vis_im
-            im = fac_re * vis_im - fac_im * vis_re
-            sums.append((jnp.sum(re, axis=2, keepdims=True), jnp.sum(im, axis=2, keepdims=True)))
         acc = list(acc)
-        for j in range(block):
-            here = lanes == first + j
-            for ri in range(2):
-                for pair in range(K // 2):
-                    at = ri * 2 + pair
-                    acc[at] = jnp.where(here, sums[pair][ri][j], acc[at])
+        for j in range(BLOCK):
+            at_freq = i * (BLOCK // 2) + j // 2
+            fac_ref, row = (own_ref, 2 * at_freq + core) if j % 2 == 0 else (other_ref, at_freq)
+            vis = vis_ref[2 * at_freq + (core if j % 2 == 0 else 1 - core)].astype(F32)
+            swapped = pltpu.roll(vis, CAP, 0)
+            vis_re = jnp.where(top[0], vis, swapped)
+            vis_im = jnp.where(top[0], swapped, vis)
+            here = lanes == i * BLOCK + j
+            for pair in range(K // 2):
+                fac_re = fac_ref[row, pl.ds(pair * 8, 8)].astype(F32)
+                fac_im = fac_ref[row, pl.ds(16 + pair * 8, 8)].astype(F32)
+                re = jnp.sum(fac_re * vis_re + fac_im * vis_im, axis=1, keepdims=True)
+                im = jnp.sum(fac_re * vis_im - fac_im * vis_re, axis=1, keepdims=True)
+                acc[pair] = jnp.where(here, re, acc[pair])
+                acc[2 + pair] = jnp.where(here, im, acc[2 + pair])
         return tuple(acc)
 
-    zero = jnp.zeros((2 * CAP, freqs), F32)
-    acc = lax.fori_loop(0, freqs // block, body, (zero,) * 4)
+    zero = jnp.zeros((2 * CAP, pairs), F32)
+    acc = lax.fori_loop(0, pairs // BLOCK, body, (zero,) * 4)
     for at in range(4):
         for copy in range(out_ref.shape[0]):
             out_ref[copy, pl.ds(at * 8, 8), :] = acc[at]
 
 
-def synth_kernel(part_ref, keep_ref, fac_ref, out_ref):
-    freqs, _, base = out_ref.shape
-    block = BLOCK
+def synth_kernel(core_ref, part_ref, keep_ref, own_ref, other_ref, out_ref):
+    core = core_ref[0]
+    pairs, _, base = out_ref.shape
     total = part_ref[0]
     for source in range(1, part_ref.shape[0]):
         total = total + part_ref[source]
@@ -129,23 +126,25 @@
     top = lax.broadcasted_iota(jnp.int32, (2 * CAP, base), 0) < CAP
 
     def body(i, kept):
-        first = pl.multiple_of(i * block, block)
-        for j in range(block):
+        for j in range(BLOCK):
+            at_freq = i * (BLOCK // 2) + j // 2
+            fac_ref, row = (own_ref, 2 * at_freq + core) if j % 2 == 0 else (other_ref, at_freq)
             re = jnp.zeros((2 * CAP, base), F32)
             im = jnp.zeros((2 * CAP, base), F32)
             for pair in range(K // 2):
-                fac_re = fac_ref[first + j, pl.ds(pair * 8, 8)].astype(F32)
-                fac_im = fac_ref[first + j, pl.ds(16 + pair * 8, 8)].astype(F32)
+                fac_re = fac_ref[row, pl.ds(pair * 8, 8)].astype(F32)
+                fac_im = fac_ref[row, pl.ds(16 + pair * 8, 8)].astype(F32)
                 kept_re = kept[pair * 8 : pair * 8 + 8, j : j + 1]
                 kept_im = kept[16 + pair * 8 : 24 + pair * 8, j : j + 1]
                 re = re + (fac_re * kept_re - fac_im * kept_im)
                 im = im + (fac_re * kept_im + fac_im * kept_re)
             re = re + pltpu.roll(re, CAP, 0)
             im = im + pltpu.roll(im, CAP, 0)
-            out_ref[first + j] = jnp.where(top, re, im).astype(BF16)
-        return pltpu.roll(kept, freqs - block, 1)
-
-    lax.fori_loop(0, freqs // block, body, kept)
+            filtered = jnp.where(top, re, im).astype(BF16)
+            out_ref[2 * at_freq + (core if j % 2 == 0 else 1 - core)] = filtered
+        return pltpu.roll(kept, pairs - BLOCK, 1)
+
+    lax.fori_loop(0, pairs // BLOCK, body, kept)
 
 
 def final_kernel(target_ref, slots_ref, out_ref):
@@ -183,32 +182,61 @@
         compiler_params=pltpu.CompilerParams(vmem_limit_bytes=40 << 20),
         name="dft",
     )(*(pltpu.with_memory_space_constraint(a, pltpu.HBM) for a in (owner_row, flat, wave)))
-    incoming = lax.all_to_all(
-        outgoing.reshape(n_freq, width, base), "freq", split_axis=0, concat_axis=0, tiled=True
-    )
-
-    slot_rows = myself * width + jnp.arange(CAP, dtype=jnp.int32)
-    mine = (target == slot_rows[:, None]).astype(BF16)
+    n_chip = n_freq // 2
+    alike = [[2 * chip + side for chip in range(n_chip)] for side in range(2)]
+    swap = [(d, d ^ 1) for d in range(n_freq)]
+    chip, core = myself >> 1, myself & 1
+
+    def exchange(rows):
+        return lax.all_to_all(
+            rows.reshape(n_chip, 2 * width, base),
+            "freq",
+            split_axis=0,
+            concat_axis=0,
+            axis_index_groups=alike,
+            tiled=True,
+        ).reshape(n_freq, width, base)
+
+    incoming = exchange(outgoing)
+
+    factors, _ = lax.optimization_barrier((factors, outgoing))
+    by_freq = jnp.transpose(factors, (1, 2, 3, 0, 4)).reshape(n_freq, 2 * K * CAP, base)
+    sent = lax.dynamic_slice_in_dim(
+        by_freq.reshape(n_chip, 2, 2 * K * CAP, base), 1 - core, 1, 1
+    ).reshape(n_chip, 2 * K * CAP, base)
+    other = lax.ppermute(sent, "freq", swap)
+
+    side = jnp.arange(2, dtype=jnp.int32)[:, None]
+    slot_rows = (2 * chip + (core ^ side)) * width + jnp.arange(CAP, dtype=jnp.int32)
+    mine = (target == slot_rows.reshape(2 * CAP, 1)).astype(BF16)
     limits = jnp.dot(mine, counts.astype(BF16), preferred_element_type=F32)
-    by_freq = jnp.transpose(factors, (1, 2, 3, 0, 4)).reshape(n_freq, 2 * K * CAP, base)
-
+    lane = jnp.arange(n_freq, dtype=jnp.int32)
+    chosen = (lane[:, None] == (lane & -2) + core).astype(BF16)
+    limits = jnp.dot(limits.astype(BF16), chosen, preferred_element_type=F32)
+    limits = jnp.where(lane & 1 == 0, limits[:CAP], limits[CAP:])
+
+    core_word = core.reshape(1)
+    smem = pl.BlockSpec(memory_space=pltpu.SMEM)
+    vmem = pl.BlockSpec(memory_space=pltpu.VMEM)
     partial, keep = pl.pallas_call(
         coef_kernel,
+        in_specs=[smem, vmem, vmem, vmem, vmem],
         out_shape=[
             jax.ShapeDtypeStruct((n_bl, 2 * K * CAP, n_freq), F32),
             jax.ShapeDtypeStruct((2 * K * CAP, n_freq), F32),
         ],
         compiler_params=pltpu.CompilerParams(vmem_limit_bytes=40 << 20),
         name="coef",
-    )(incoming, by_freq, limits)
+    )(core_word, incoming, by_freq, other, limits)
     partials = lax.all_to_all(partial, "bl", split_axis=0, concat_axis=0, tiled=True)
     synthesis = pl.pallas_call(
         synth_kernel,
+        in_specs=[smem, vmem, vmem, vmem, vmem],
         out_shape=jax.ShapeDtypeStruct((n_freq, width, base), BF16),
         compiler_params=pltpu.CompilerParams(vmem_limit_bytes=40 << 20),
         name="synth",
-    )(partials, keep, by_freq)
-    returned = lax.all_to_all(synthesis, "freq", split_axis=0, concat_axis=0, tiled=True)
+    )(core_word, partials, keep, by_freq, other)
+    returned = exchange(synthesis)
     filtered = pl.pallas_call(
         final_kernel,
         out_shape=jax.ShapeDtypeStruct((2, base, MM), BF16),

time: 113 us -> 107 us (0.947)
  waiting for transfers between devices: 25.2 us -> 17.7 us
  local copies, waits for them, and re-layouts: 6.62 us -> 11.5 us
  blocking collectives: 50.1 us -> 45.8 us
    all_to_all x1, waiting for transfers between devices: 25.2 us -> 17.7 us  [exchange(): lax.all_to_all(rows.reshape(n_chip, 2 * width, base), 'freq', split_axis=...]
    all_to_all x1, blocking collectives: 40.2 us -> 35.9 us  [exchange(): lax.all_to_all(rows.reshape(n_chip, 2 * width, base), 'freq', split_axis=...]
    reshape x0 -> x1, local copies, waits for them, and re-layouts: none -> 2.28 us  [local(): sent = lax.dynamic_slice_in_dim(by_freq.reshape(n_chip, 2, 2 * K * CAP, b...]
    another operation x0 -> x1, local copies, waits for them, and re-layouts: none -> 2.23 us  [local(): by_freq.reshape(n_chip, 2, 2 * K * CAP, base)]
    ppermute x0 -> x1, starting transfers between devices: none -> 1.91 us  [local(): other = lax.ppermute(sent, 'freq', swap)]
  transfers between devices with their start and end apart: 1 -> 2, of which waited for: 1 -> 1; matrix products, arithmetic and copies ran while one was open for 6% -> 11% of each run, Pallas kernels for 0% -> 0%
where the time goes in v3:
time: 107 us; the launch traced here: 106 us
  blocking collectives  45.8 us (43%)
  starting transfers between devices  20.9 us (20%)
  waiting for transfers between devices  17.7 us (17%)
  local copies, waits for them, and re-layouts  11.5 us (11%)
  Pallas kernels  9.97 us (9%)
    all_to_all x1, blocking collectives, exchange(): lax.all_to_all(rows.reshape(n_chip, 2 * width, base), 'freq', split_axis=...  35.9 us
    all_to_all x1, starting transfers between devices, exchange(): lax.all_to_all(rows.reshape(n_chip, 2 * width, base), 'freq', split_axis=...  19 us
    all_to_all x1, waiting for transfers between devices, exchange(): lax.all_to_all(rows.reshape(n_chip, 2 * width, base), 'freq', split_axis=...  17.7 us
    all_to_all x1, blocking collectives, local(): lax.all_to_all(partial, 'bl', split_axis=0, concat_axis=0, tiled=True)  9.89 us
    pallas_call x1, Pallas kernels, local(): pl.pallas_call(dft_kernel, in_specs=[hbm, hbm, hbm], out_shape=[jax.Shape...  5.12 us
    transpose x1, local copies, waits for them, and re-layouts, local(): jnp.transpose(factors, (1, 2, 3, 0, 4)).reshape(n_freq, 2 * K * CAP, base)  4.29 us
    reshape x1, local copies, waits for them, and re-layouts, local(): jnp.transpose(factors, (1, 2, 3, 0, 4)).reshape(n_freq, 2 * K * CAP, base)  2.59 us
    reshape x1, local copies, waits for them, and re-layouts, local(): sent = lax.dynamic_slice_in_dim(by_freq.reshape(n_chip, 2, 2 * K * CAP, b...  2.28 us
  transfers between devices with their start and end apart: 2, of which 1 were waited for; matrix products, arithmetic and copies ran while one was open for 11% of the time, Pallas kernels for 0%

profile of v3, /device:TPU:6, one launch (start us, length us, event | category | flops | bytes accessed | tf_op | source)
XLA Modules:
  0.0 106.4 jit_solution(9115311986138932091)
XLA Ops:
  0.0 5.1 %dft.1 = (bf16[1024,256]{1,0:T(8,128)(2,1)}, s32[1,384]{1,0:T(1,128)S(1)}) custom-call(s32[1,384]{1,0:T(1,128)} %bitcast.15, bf16[512,2048]{1,0:T(8,128)(2,1)} %bitcast.13, bf16[1024,768]{1,0:T(8,128)(2,1)} %constant.22.clone.wave_hbm), custom_call_target="tpu_custom_call" | custom-call | tf_op jit(solution)/shard_map/dft/pallas_call | solution.py:169
  5.1 19.0 %all-to-all-start = ((bf16[64,16,256]{2,1,0:T(8,128)(2,1)}), bf16[64,16,256]{2,1,0:T(8,128)(2,1)}, u32[]{:S(2)}, u32[]{:S(2)}) async-start(bf16[64,16,256]{2,1,0:T(8,128)(2,1)} %bitcast.3), calls=%async_computation | async-start | bytes 1048576 | tf_op jit(solution)/shard_map/all_to_all | solution.py:191
  24.1 4.3 %copy.7 = bf16[128,2,4,4,256]{4,3,2,1,0:T(4,128)(2,1)S(1)} copy(bf16[128,2,4,4,256]{4,2,1,0,3:T(4,128)(2,1)} %bitcast.14) | data formatting | bytes 4194304 | tf_op jit(solution)/shard_map/transpose | solution.py:203
  28.4 0.0 copy-start
  28.4 2.2 %reshape_reshape.6 = bf16[64,2,32,256]{3,2,1,0:T(8,128)(2,1)} reshape(bf16[128,2,4,4,256]{4,3,2,1,0:T(4,128)(2,1)S(1)} %copy.7) | data formatting | bytes 4194304 | tf_op jit(solution)/shard_map/reshape;reshape | solution.py:205
  30.7 0.0 copy-done
  30.7 2.3 %dynamic-slice_bitcast_fusion = bf16[64,32,256]{2,1,0:T(8,128)(2,1)} fusion(bf16[64,2,32,256]{3,2,1,0:T(8,128)(2,1)} %reshape_reshape.6, s32[]{:T(128)S(6)} %select_n.7), kind=kLoop, calls=%fused_computation.2 | loop fusion | bytes 2097156 | tf_op jit(solution)/shard_map/reshape | solution.py:206
  33.0 1.9 %collective-permute-start = (bf16[64,32,256]{2,1,0:T(8,128)(2,1)}, bf16[64,32,256]{2,1,0:T(8,128)(2,1)S(1)}, u32[]{:S(2)}, u32[]{:S(2)}) collective-permute-start(bf16[64,32,256]{2,1,0:T(8,128)(2,1)} %dynamic-slice_bitcast_fusion), channel_id=1, source_target_pairs={{0,4},{4,0},{8,12},{12,8},{16,20},{20,16},{24,28},{28,24},{32,36},... | collective-permute-start | bytes 3145736 | tf_op jit(solution)/shard_map/ppermute | solution.py:207
  34.9 0.0 copy-start.1
  34.9 2.6 %reshape.58.own_ref = bf16[128,32,256]{2,1,0:T(8,128)(2,1)S(1)} reshape(bf16[128,2,4,4,256]{4,3,2,1,0:T(4,128)(2,1)} %copy-done) | data formatting | bytes 4194304 | tf_op jit(solution)/shard_map/reshape | solution.py:203
  37.5 0.1 iota_add_fusion
  37.6 0.1 add.51
  37.7 0.0 copy-done.1
  37.7 0.3 fusion
  38.0 0.0 collective-permute-done.other_ref
  38.0 17.7 %all-to-all-done = bf16[64,16,256]{2,1,0:T(8,128)(2,1)} async-done(((bf16[64,16,256]{2,1,0:T(8,128)(2,1)}), bf16[64,16,256]{2,1,0:T(8,128)(2,1)}, u32[]{:S(2)}, u32[]{:S(2)}) %all-to-all-start) | async-done | bytes 524320 | tf_op jit(solution)/shard_map/all_to_all | solution.py:191
  55.7 2.2 %coef.1 = (f32[4,32,128]{2,1,0:T(8,128)S(1)}, f32[32,128]{1,0:T(8,128)S(1)}) custom-call(s32[1]{0:T(128)} %bitcast.2.core_ref, bf16[128,8,256]{2,1,0:T(8,128)(2,1)} %bitcast.4.vis_ref, bf16[128,32,256]{2,1,0:T(8,128)(2,1)S(1)} %reshape.58.own_ref, bf16[64,32,256]{2,1,0:T(8,128)(2,1)S(1)} %collective-permute-done.other_ref, ...), custom_call_target="tpu_custom_call" | custom-call | tf_op jit(solution)/shard_map/coef/pallas_call | solution.py:221
  57.9 9.9 %all_to_all.15.part_ref = f32[4,32,128]{2,1,0:T(8,128)S(1)} all-to-all(f32[4,32,128]{2,1,0:T(8,128)S(1)} %get-tuple-element.13), channel_id=1, replica_groups=mesh['freq'=128,'bl'=4] {'bl'}, dimensions={0} | all-to-all | bytes 131072 | tf_op jit(solution)/shard_map/all_to_all | solution.py:231
  67.8 1.2 %synth.1 = bf16[128,8,256]{2,1,0:T(8,128)(2,1)S(1)} custom-call(s32[1]{0:T(128)} %bitcast.2.core_ref, f32[4,32,128]{2,1,0:T(8,128)S(1)} %all_to_all.15.part_ref, f32[32,128]{1,0:T(8,128)S(1)} %get-tuple-element.14.keep_ref, bf16[128,32,256]{2,1,0:T(8,128)(2,1)S(1)} %reshape.58.own_ref, bf16[64,32,256]{2,1,0:T(8,128)(2,1)S(1)} %collective-permute-done.other_ref), custom_call_target="tpu_custom_call" | custom-call | tf_op jit(solution)/shard_map/synth/pallas_call | solution.py:232
  68.9 35.9 %all_to_all.16 = bf16[64,16,256]{2,1,0:T(8,128)(2,1)S(1)} all-to-all(bf16[64,16,256]{2,1,0:T(8,128)(2,1)S(1)} %bitcast.12), channel_id=1, replica_groups={{0,8,16,24,32,40,48,56,64,72,80,88,96,104,112,120,128,136,144,152,160,1..., dimensions={0} | all-to-all | bytes 1048576 | tf_op jit(solution)/shard_map/all_to_all | solution.py:191
  104.9 1.5 %final.1 = bf16[2,256,384]{2,1,0:T(8,128)(2,1)} custom-call(s32[1,384]{1,0:T(1,128)S(1)} %get-tuple-element.10.target_ref, bf16[1024,256]{1,0:T(8,128)(2,1)S(1)} %bitcast.11), custom_call_target="tpu_custom_call" | custom-call | tf_op jit(solution)/shard_map/final/pallas_call | solution.py:240
  (5 shorter events, 0.0 us)
Async XLA Ops:
  5.1 50.6 %all-to-all-start = ((bf16[64,16,256]{2,1,0:T(8,128)(2,1)}), bf16[64,16,256]{2,1,0:T(8,128)(2,1)}, u32[]{:S(2)}, u32[]{:S(2)}) async-start(bf16[64,16,256]{2,1,0:T(8,128)(2,1)} %bitcast.3), calls=%async_computation | async-start | bytes 1048576 | tf_op jit(solution)/shard_map/all_to_all | solution.py:191
  28.4 2.2 %copy-start = (bf16[128,2,4,4,256]{4,3,2,1,0:T(4,128)(2,1)}, bf16[128,2,4,4,256]{4,3,2,1,0:T(4,128)(2,1)S(1)}, u32[]{:S(2)}) copy-start(bf16[128,2,4,4,256]{4,3,2,1,0:T(4,128)(2,1)S(1)} %copy.7) | copy-start | bytes 6291460
  33.0 5.1 %collective-permute-start = (bf16[64,32,256]{2,1,0:T(8,128)(2,1)}, bf16[64,32,256]{2,1,0:T(8,128)(2,1)S(1)}, u32[]{:S(2)}, u32[]{:S(2)}) collective-permute-start(bf16[64,32,256]{2,1,0:T(8,128)(2,1)} %dynamic-slice_bitcast_fusion), channel_id=1, source_target_pairs={{0,4},{4,0},{8,12},{12,8},{16,20},{20,16},{24,28},{28,24},{32,36},... | collective-permute-start | bytes 3145736 | tf_op jit(solution)/shard_map/ppermute | solution.py:207
  34.9 2.8 %copy-start.1 = (s32[384,128]{1,0:T(8,128)S(1)}, s32[384,128]{1,0:T(8,128)}, u32[]{:S(2)}) copy-start(s32[384,128]{1,0:T(8,128)} %param.7) | copy-start | bytes 589828

commit v4 on v3

--- a/solution.py
+++ b/solution.py
@@ -80,6 +80,23 @@
     ).astype(BF16)
 
 
+def relay_kernel(core_ref, fac_ref, own_ref, sent_ref, rows_ref):
+    core = core_ref[0]
+
+    def body(i, carry):
+        for out_ref, side in ((own_ref, core), (sent_ref, 1 - core)):
+            for lane in range(rows_ref.shape[0]):
+                for part in range(2):
+                    for slot in range(CAP):
+                        rows = fac_ref[slot, 2 * i + side, part, :, pl.ds(lane * 128, 128)]
+                        first = part * K * CAP + slot
+                        rows_ref[lane, pl.ds(first, K, stride=CAP), :] = rows.astype(F32)
+                out_ref[i, :, pl.ds(lane * 128, 128)] = rows_ref[lane].astype(BF16)
+        return carry
+
+    lax.fori_loop(0, own_ref.shape[0], body, 0, unroll=4)
+
+
 def coef_kernel(core_ref, vis_ref, own_ref, other_ref, limit_ref, out_ref, keep_ref):
     core = core_ref[0]
     pairs, _, base = vis_ref.shape
@@ -93,15 +110,15 @@
         acc = list(acc)
         for j in range(BLOCK):
             at_freq = i * (BLOCK // 2) + j // 2
-            fac_ref, row = (own_ref, 2 * at_freq + core) if j % 2 == 0 else (other_ref, at_freq)
+            fac_ref = own_ref if j % 2 == 0 else other_ref
             vis = vis_ref[2 * at_freq + (core if j % 2 == 0 else 1 - core)].astype(F32)
             swapped = pltpu.roll(vis, CAP, 0)
             vis_re = jnp.where(top[0], vis, swapped)
             vis_im = jnp.where(top[0], swapped, vis)
             here = lanes == i * BLOCK + j
             for pair in range(K // 2):
-                fac_re = fac_ref[row, pl.ds(pair * 8, 8)].astype(F32)
-                fac_im = fac_ref[row, pl.ds(16 + pair * 8, 8)].astype(F32)
+                fac_re = fac_ref[at_freq, pl.ds(pair * 8, 8)].astype(F32)
+                fac_im = fac_ref[at_freq, pl.ds(16 + pair * 8, 8)].astype(F32)
                 re = jnp.sum(fac_re * vis_re + fac_im * vis_im, axis=1, keepdims=True)
                 im = jnp.sum(fac_re * vis_im - fac_im * vis_re, axis=1, keepdims=True)
                 acc[pair] = jnp.where(here, re, acc[pair])
@@ -128,12 +145,12 @@
     def body(i, kept):
         for j in range(BLOCK):
             at_freq = i * (BLOCK // 2) + j // 2
-            fac_ref, row = (own_ref, 2 * at_freq + core) if j % 2 == 0 else (other_ref, at_freq)
+            fac_ref = own_ref if j % 2 == 0 else other_ref
             re = jnp.zeros((2 * CAP, base), F32)
             im = jnp.zeros((2 * CAP, base), F32)
             for pair in range(K // 2):
-                fac_re = fac_ref[row, pl.ds(pair * 8, 8)].astype(F32)
-                fac_im = fac_ref[row, pl.ds(16 + pair * 8, 8)].astype(F32)
+                fac_re = fac_ref[at_freq, pl.ds(pair * 8, 8)].astype(F32)
+                fac_im = fac_ref[at_freq, pl.ds(16 + pair * 8, 8)].astype(F32)
                 kept_re = kept[pair * 8 : pair * 8 + 8, j : j + 1]
                 kept_im = kept[16 + pair * 8 : 24 + pair * 8, j : j + 1]
                 re = re + (fac_re * kept_re - fac_im * kept_im)
@@ -147,19 +164,25 @@
     lax.fori_loop(0, pairs // BLOCK, body, kept)
 
 
-def final_kernel(target_ref, slots_ref, out_ref):
+def final_kernel(target_ref, slots_ref, out_hbm, out_ref, sems):
     rows = lax.broadcasted_iota(jnp.int32, (slots_ref.shape[0], MM), 0)
+    copies = []
     for part in range(2):
         placing = jnp.where(rows == target_ref[...] + part * CAP, 1.0, 0.0).astype(BF16)
         out_ref[part] = lax.dot_general(
             slots_ref[...], placing, (((0,), (0,)), ((), ())), preferred_element_type=F32
         ).astype(BF16)
+        copies.append(pltpu.make_async_copy(out_ref.at[part], out_hbm.at[part], sems.at[part]))
+        copies[part].start()
+    for copy in copies:
+        copy.wait()
 
 
 def local(vis_time, owner, counts, factors):
-    n_freq = lax.axis_size("freq")
+    n_chip = lax.axis_size("chip")
+    n_freq = n_chip * lax.axis_size("core")
     n_bl = lax.axis_size("bl")
-    myself = lax.axis_index("freq")
+    chip, core = lax.axis_index("chip"), lax.axis_index("core")
     base = vis_time.shape[2]
     flat = vis_time.reshape(2 * base, NT)
     owner_row = owner.reshape(1, MM)
@@ -179,32 +202,31 @@
             pltpu.VMEM((2, CHUNK, 2 * MM), BF16),
             pltpu.SemaphoreType.DMA((7,)),
         ],
-        compiler_params=pltpu.CompilerParams(vmem_limit_bytes=40 << 20),
+        compiler_params=pltpu.CompilerParams(vmem_limit_bytes=24 << 20),
         name="dft",
     )(*(pltpu.with_memory_space_constraint(a, pltpu.HBM) for a in (owner_row, flat, wave)))
-    n_chip = n_freq // 2
-    alike = [[2 * chip + side for chip in range(n_chip)] for side in range(2)]
-    swap = [(d, d ^ 1) for d in range(n_freq)]
-    chip, core = myself >> 1, myself & 1
-
     def exchange(rows):
         return lax.all_to_all(
-            rows.reshape(n_chip, 2 * width, base),
-            "freq",
-            split_axis=0,
-            concat_axis=0,
-            axis_index_groups=alike,
-            tiled=True,
+            rows.reshape(n_chip, 2 * width, base), "chip", split_axis=0, concat_axis=0, tiled=True
         ).reshape(n_freq, width, base)
 
     incoming = exchange(outgoing)
 
     factors, _ = lax.optimization_barrier((factors, outgoing))
-    by_freq = jnp.transpose(factors, (1, 2, 3, 0, 4)).reshape(n_freq, 2 * K * CAP, base)
-    sent = lax.dynamic_slice_in_dim(
-        by_freq.reshape(n_chip, 2, 2 * K * CAP, base), 1 - core, 1, 1
-    ).reshape(n_chip, 2 * K * CAP, base)
-    other = lax.ppermute(sent, "freq", swap)
+    core_word = core.reshape(1)
+    smem = pl.BlockSpec(memory_space=pltpu.SMEM)
+    vmem = pl.BlockSpec(memory_space=pltpu.VMEM)
+    own, sent = pl.pallas_call(
+        relay_kernel,
+        grid=(4,),
+        in_specs=[smem, pl.BlockSpec((CAP, n_freq // 4, 2, K, base), lambda i: (0, i, 0, 0, 0))],
+        out_specs=[pl.BlockSpec((n_chip // 4, 2 * K * CAP, base), lambda i: (i, 0, 0))] * 2,
+        out_shape=[jax.ShapeDtypeStruct((n_chip, 2 * K * CAP, base), BF16)] * 2,
+        scratch_shapes=[pltpu.VMEM((base // 128, 2 * K * CAP, 128), F32)],
+        compiler_params=pltpu.CompilerParams(vmem_limit_bytes=8 << 20),
+        name="relay",
+    )(core_word, pltpu.with_memory_space_constraint(factors, pltpu.HBM))
+    other = lax.ppermute(sent, "core", [(0, 1), (1, 0)])
 
     side = jnp.arange(2, dtype=jnp.int32)[:, None]
     slot_rows = (2 * chip + (core ^ side)) * width + jnp.arange(CAP, dtype=jnp.int32)
@@ -215,9 +237,6 @@
     limits = jnp.dot(limits.astype(BF16), chosen, preferred_element_type=F32)
     limits = jnp.where(lane & 1 == 0, limits[:CAP], limits[CAP:])
 
-    core_word = core.reshape(1)
-    smem = pl.BlockSpec(memory_space=pltpu.SMEM)
-    vmem = pl.BlockSpec(memory_space=pltpu.VMEM)
     partial, keep = pl.pallas_call(
         coef_kernel,
         in_specs=[smem, vmem, vmem, vmem, vmem],
@@ -225,29 +244,36 @@
             jax.ShapeDtypeStruct((n_bl, 2 * K * CAP, n_freq), F32),
             jax.ShapeDtypeStruct((2 * K * CAP, n_freq), F32),
         ],
-        compiler_params=pltpu.CompilerParams(vmem_limit_bytes=40 << 20),
+        compiler_params=pltpu.CompilerParams(vmem_limit_bytes=8 << 20),
         name="coef",
-    )(core_word, incoming, by_freq, other, limits)
+    )(core_word, incoming, own, other, limits)
     partials = lax.all_to_all(partial, "bl", split_axis=0, concat_axis=0, tiled=True)
     synthesis = pl.pallas_call(
         synth_kernel,
         in_specs=[smem, vmem, vmem, vmem, vmem],
         out_shape=jax.ShapeDtypeStruct((n_freq, width, base), BF16),
-        compiler_params=pltpu.CompilerParams(vmem_limit_bytes=40 << 20),
+        compiler_params=pltpu.CompilerParams(vmem_limit_bytes=8 << 20),
         name="synth",
-    )(core_word, partials, keep, by_freq, other)
+    )(core_word, partials, keep, own, other)
     returned = exchange(synthesis)
     filtered = pl.pallas_call(
         final_kernel,
+        out_specs=hbm,
         out_shape=jax.ShapeDtypeStruct((2, base, MM), BF16),
-        compiler_params=pltpu.CompilerParams(vmem_limit_bytes=40 << 20),
+        scratch_shapes=[pltpu.VMEM((2, base, MM), BF16), pltpu.SemaphoreType.DMA((2,))],
+        compiler_params=pltpu.CompilerParams(vmem_limit_bytes=16 << 20),
         name="final",
     )(target, returned.reshape(n_freq * width, base))
     return filtered[None]
 
 
 def solution(mesh):
-    placed = (P("freq", None, "bl", None), P(), P(), P("freq", None, None, None, "bl"))
+    n_freq, n_bl = mesh.devices.shape
+    by_chip = jax.sharding.Mesh(
+        mesh.devices.reshape(n_freq // 2, 2, n_bl), ("chip", "core", "bl")
+    )
+    freq = ("chip", "core")
+    placed = (P(freq, None, "bl", None), P(), P(), P(freq, None, None, None, "bl"))
     return jax.shard_map(
-        local, mesh=mesh, in_specs=placed, out_specs=P("freq", None, "bl", None), check_vma=False
+        local, mesh=by_chip, in_specs=placed, out_specs=P(freq, None, "bl", None), check_vma=False
     )

time: 107 us -> 106 us (level)
  local copies, waits for them, and re-layouts: 11.5 us -> 0.09 us
  waiting for transfers between devices: 17.7 us -> 24.9 us
  Pallas kernels: 9.97 us -> 13.2 us
    all_to_all x1, waiting for transfers between devices: 17.7 us -> 22.6 us  [exchange(): lax.all_to_all(rows.reshape(n_chip, 2 * width, base), 'chip', split_axis=...]
    reshape x2 -> x0, local copies, waits for them, and re-layouts: 4.87 us -> none  [the longest x1 2.59 us: local(): jnp.transpose(factors, (1, 2, 3, 0, 4)).reshape(n_freq, 2 * K * CAP, base)]
    transpose x1 -> x0, local copies, waits for them, and re-layouts: 4.29 us -> none  [local(): jnp.transpose(factors, (1, 2, 3, 0, 4)).reshape(n_freq, 2 * K * CAP, base)]
    pallas_call x1 -> x2, Pallas kernels: 1.53 us -> 5.76 us  [the longest x1 4.3 us: local(): pl.pallas_call(relay_kernel, grid=(4,), in_specs=[smem, pl.BlockSpec((CAP...]
    ppermute x1, waiting for transfers between devices: 0.01 us -> 2.31 us  [local(): other = lax.ppermute(sent, 'core', [(0, 1), (1, 0)])]
    another operation x1 -> x0, local copies, waits for them, and re-layouts: 2.23 us -> none  [local(): by_freq.reshape(n_chip, 2, 2 * K * CAP, base)]
  transfers between devices with their start and end apart: 2 -> 2, of which waited for: 1 -> 2; matrix products, arithmetic and copies ran while one was open for 11% -> 0% of each run, Pallas kernels for 0% -> 4%
where the time goes in v4:
time: 106 us; the launch traced here: 105 us
  blocking collectives  45.8 us (43%)
  waiting for transfers between devices  24.9 us (23%)
  starting transfers between devices  20.8 us (20%)
  Pallas kernels  13.2 us (12%)
    all_to_all x1, blocking collectives, exchange(): lax.all_to_all(rows.reshape(n_chip, 2 * width, base), 'chip', split_axis=...  35.9 us
    all_to_all x1, waiting for transfers between devices, exchange(): lax.all_to_all(rows.reshape(n_chip, 2 * width, base), 'chip', split_axis=...  22.6 us
    all_to_all x1, starting transfers between devices, exchange(): lax.all_to_all(rows.reshape(n_chip, 2 * width, base), 'chip', split_axis=...  18.9 us
    all_to_all x1, blocking collectives, local(): lax.all_to_all(partial, 'bl', split_axis=0, concat_axis=0, tiled=True)  9.89 us
    pallas_call x1, Pallas kernels, local(): pl.pallas_call(dft_kernel, in_specs=[hbm, hbm, hbm], out_shape=[jax.Shape...  5.13 us
    pallas_call x1, Pallas kernels, local(): pl.pallas_call(relay_kernel, grid=(4,), in_specs=[smem, pl.BlockSpec((CAP...  4.3 us
    ppermute x1, waiting for transfers between devices, local(): other = lax.ppermute(sent, 'core', [(0, 1), (1, 0)])  2.31 us
  transfers between devices with their start and end apart: 2, of which 2 were waited for; matrix products, arithmetic and copies ran while one was open for 0% of the time, Pallas kernels for 4%

profile of v4, /device:TPU:6, one launch (start us, length us, event | category | flops | bytes accessed | tf_op | source)
XLA Modules:
  0.0 105.3 jit_solution(14075272863942744537)
XLA Ops:
  0.0 5.1 %dft.1 = (bf16[1024,256]{1,0:T(8,128)(2,1)}, s32[1,384]{1,0:T(1,128)S(1)}) custom-call(s32[1,384]{1,0:T(1,128)} %bitcast.12, bf16[512,2048]{1,0:T(8,128)(2,1)} %bitcast.11, bf16[1024,768]{1,0:T(8,128)(2,1)} %constant.24.clone.wave_hbm), custom_call_target="tpu_custom_call" | custom-call | tf_op jit(solution)/shard_map/dft/pallas_call | solution.py:192
  5.1 0.0 copy-start
  5.1 18.9 %all-to-all-start = ((bf16[64,16,256]{2,1,0:T(8,128)(2,1)}), bf16[64,16,256]{2,1,0:T(8,128)(2,1)S(1)}, u32[]{:S(2)}, u32[]{:S(2)}) async-start(bf16[64,16,256]{2,1,0:T(8,128)(2,1)} %bitcast.3), calls=%async_computation | async-start | bytes 1048576 | tf_op jit(solution)/shard_map/all_to_all | solution.py:209
  24.1 4.3 %relay.1 = (bf16[64,32,256]{2,1,0:T(8,128)(2,1)S(1)}, bf16[64,32,256]{2,1,0:T(8,128)(2,1)}) custom-call(s32[1]{0:T(128)} %bitcast.2.core_ref, bf16[4,128,2,4,256]{4,3,2,1,0:T(4,128)(2,1)} %fac_ref), custom_call_target="tpu_custom_call" | custom-call | tf_op jit(solution)/shard_map/relay/pallas_call | solution.py:219
  28.4 1.9 %collective-permute-start = (bf16[64,32,256]{2,1,0:T(8,128)(2,1)}, bf16[64,32,256]{2,1,0:T(8,128)(2,1)S(1)}, u32[]{:S(2)}, u32[]{:S(2)}) collective-permute-start(bf16[64,32,256]{2,1,0:T(8,128)(2,1)} %get-tuple-element.16), channel_id=1, source_target_pairs={{0,4},{4,0},{1,5},{5,1},{2,6},{6,2},{3,7},{7,3},{8,12},{12,8},{9,1... | collective-permute-start | bytes 3145736 | tf_op jit(solution)/shard_map/ppermute | solution.py:229
  30.3 0.1 iota_add_fusion
  30.4 0.1 add.46
  30.5 0.0 copy-done
  30.5 0.3 fusion
  30.8 2.3 %collective-permute-done.other_ref = bf16[64,32,256]{2,1,0:T(8,128)(2,1)S(1)} collective-permute-done((bf16[64,32,256]{2,1,0:T(8,128)(2,1)}, bf16[64,32,256]{2,1,0:T(8,128)(2,1)S(1)}, u32[]{:S(2)}, u32[]{:S(2)}) %collective-permute-start) | collective-permute-done | bytes 1048608 | tf_op jit(solution)/shard_map/ppermute | solution.py:229
  33.1 22.6 %all-to-all-done = bf16[64,16,256]{2,1,0:T(8,128)(2,1)S(1)} async-done(((bf16[64,16,256]{2,1,0:T(8,128)(2,1)}), bf16[64,16,256]{2,1,0:T(8,128)(2,1)S(1)}, u32[]{:S(2)}, u32[]{:S(2)}) %all-to-all-start) | async-done | bytes 524320 | tf_op jit(solution)/shard_map/all_to_all | solution.py:209
  55.8 1.1 %coef.1 = (f32[4,32,128]{2,1,0:T(8,128)S(1)}, f32[32,128]{1,0:T(8,128)S(1)}) custom-call(s32[1]{0:T(128)} %bitcast.2.core_ref, bf16[128,8,256]{2,1,0:T(8,128)(2,1)S(1)} %bitcast.8, bf16[64,32,256]{2,1,0:T(8,128)(2,1)S(1)} %get-tuple-element.15.own_ref, bf16[64,32,256]{2,1,0:T(8,128)(2,1)S(1)} %collective-permute-done.other_ref, ...), custom_call_target="tpu_custom_call" | custom-call | tf_op jit(solution)/shard_map/coef/pallas_call | solution.py:240
  56.9 9.9 %all_to_all.15.part_ref = f32[4,32,128]{2,1,0:T(8,128)S(1)} all-to-all(f32[4,32,128]{2,1,0:T(8,128)S(1)} %get-tuple-element.17), channel_id=1, replica_groups=mesh['chip'=64,'core'=2,'bl'=4] {'bl'}, dimensions={0} | all-to-all | bytes 131072 | tf_op jit(solution)/shard_map/all_to_all | solution.py:250
  66.8 1.2 %synth.1 = bf16[128,8,256]{2,1,0:T(8,128)(2,1)S(1)} custom-call(s32[1]{0:T(128)} %bitcast.2.core_ref, f32[4,32,128]{2,1,0:T(8,128)S(1)} %all_to_all.15.part_ref, f32[32,128]{1,0:T(8,128)S(1)} %get-tuple-element.18.keep_ref, bf16[64,32,256]{2,1,0:T(8,128)(2,1)S(1)} %get-tuple-element.15.own_ref, bf16[64,32,256]{2,1,0:T(8,128)(2,1)S(1)} %collective-permute-done.other_ref), custom_call_target="tpu_custom_call" | custom-call | tf_op jit(solution)/shard_map/synth/pallas_call | solution.py:251
  67.9 35.9 %all_to_all.16 = bf16[64,16,256]{2,1,0:T(8,128)(2,1)S(1)} all-to-all(bf16[64,16,256]{2,1,0:T(8,128)(2,1)S(1)} %bitcast.10), channel_id=1, replica_groups=mesh['chip'=64,'core'=2,'bl'=4] {'chip'}, dimensions={0} | all-to-all | bytes 1048576 | tf_op jit(solution)/shard_map/all_to_all | solution.py:209
  103.9 1.5 %final.1 = bf16[2,256,384]{2,1,0:T(8,128)(2,1)} custom-call(s32[1,384]{1,0:T(1,128)S(1)} %get-tuple-element.12.target_ref, bf16[1024,256]{1,0:T(8,128)(2,1)S(1)} %bitcast.9), custom_call_target="tpu_custom_call" | custom-call | tf_op jit(solution)/shard_map/final/pallas_call | solution.py:259
  (5 shorter events, 0.0 us)
Async XLA Ops:
  5.1 25.4 %copy-start = (s32[384,128]{1,0:T(8,128)S(1)}, s32[384,128]{1,0:T(8,128)}, u32[]{:S(2)}) copy-start(s32[384,128]{1,0:T(8,128)} %param.7) | copy-start | bytes 589828
  5.1 50.6 %all-to-all-start = ((bf16[64,16,256]{2,1,0:T(8,128)(2,1)}), bf16[64,16,256]{2,1,0:T(8,128)(2,1)S(1)}, u32[]{:S(2)}, u32[]{:S(2)}) async-start(bf16[64,16,256]{2,1,0:T(8,128)(2,1)} %bitcast.3), calls=%async_computation | async-start | bytes 1048576 | tf_op jit(solution)/shard_map/all_to_all | solution.py:209
  28.4 4.8 %collective-permute-start = (bf16[64,32,256]{2,1,0:T(8,128)(2,1)}, bf16[64,32,256]{2,1,0:T(8,128)(2,1)S(1)}, u32[]{:S(2)}, u32[]{:S(2)}) collective-permute-start(bf16[64,32,256]{2,1,0:T(8,128)(2,1)} %get-tuple-element.16), channel_id=1, source_target_pairs={{0,4},{4,0},{1,5},{5,1},{2,6},{6,2},{3,7},{7,3},{8,12},{12,8},{9,1... | collective-permute-start | bytes 3145736 | tf_op jit(solution)/shard_map/ppermute | solution.py:229

commit v5 on v4

--- a/solution.py
+++ b/solution.py
@@ -26,8 +26,11 @@
     return rows.astype(np.float32).astype(jnp.bfloat16)
 
 
-def dft_kernel(owner_hbm, vis_hbm, wave_hbm, out_ref, target_ref, owner_ref, vis_ref, wave_ref, sems):
-    owners = out_ref.shape[0] // (2 * CAP)
+def dft_kernel(
+    owner_hbm, vis_hbm, wave_hbm, out_hbm, target_ref, owner_ref, vis_ref, wave_ref, out_ref, sems
+):
+    chips, _, width, base = out_ref.shape
+    owners = chips * width // CAP
     owner_copy = pltpu.make_async_copy(owner_hbm, owner_ref, sems.at[0])
     owner_copy.start()
     wave_copies, vis_copies = [], {}
@@ -53,10 +56,9 @@
     earlier = jnp.where(earlier, 1.0, 0.0).astype(BF16)
     before = jnp.dot(hot.astype(BF16), earlier, preferred_element_type=F32)
     rank = jnp.sum(before * hot, axis=0, keepdims=True).astype(jnp.int32)
-    target = owner * (2 * CAP) + rank
+    target = owner * CAP + rank
     target_ref[...] = target
-    target = jnp.concatenate([target, target + CAP], axis=1)
-    rows = lax.broadcasted_iota(jnp.int32, (out_ref.shape[0], 2 * MM), 0)
+    rows = lax.broadcasted_iota(jnp.int32, (owners * CAP, MM), 0)
     placing = jnp.where(rows == target, 1.0, 0.0).astype(BF16)
 
     sign = 1 - 2 * (lax.broadcasted_iota(jnp.int32, (1, 2 * MM), 1) % 2)
@@ -71,13 +73,20 @@
             if half == 1:
                 product = product * sign
             spectra = product if spectra is None else spectra + product
-    base = spectra.shape[0] // 2
     real = spectra[:base, :MM] + spectra[base:, MM:]
     imag = spectra[base:, :MM] - spectra[:base, MM:]
-    modes = jnp.concatenate([real, imag], axis=1).astype(BF16)
-    out_ref[...] = lax.dot_general(
-        placing, modes, (((1,), (1,)), ((), ())), preferred_element_type=F32
-    ).astype(BF16)
+    out_copies = []
+    for part, modes in enumerate((real, imag)):
+        placed = lax.dot_general(
+            placing, modes.astype(BF16), (((1,), (1,)), ((), ())), preferred_element_type=F32
+        )
+        out_ref[:, part] = placed.astype(BF16).reshape(chips, width, base)
+        out_copies.append(
+            pltpu.make_async_copy(out_ref.at[:, part], out_hbm.at[:, part], sems.at[7 + part])
+        )
+        out_copies[part].start()
+    for copy in out_copies:
+        copy.wait()
 
 
 def relay_kernel(core_ref, fac_ref, own_ref, sent_ref, rows_ref):
@@ -99,33 +108,35 @@
 
 def coef_kernel(core_ref, vis_ref, own_ref, other_ref, limit_ref, out_ref, keep_ref):
     core = core_ref[0]
-    pairs, _, base = vis_ref.shape
-    top = lax.broadcasted_iota(jnp.int32, (1, 2 * CAP, base), 1) < CAP
-    lanes = lax.broadcasted_iota(jnp.int32, (2 * CAP, pairs), 1)
+    chips, _, width, base = vis_ref.shape
+    pairs = 2 * chips
+    mine = lax.broadcasted_iota(jnp.int32, (width, base), 0) // CAP == core
+    lanes = lax.broadcasted_iota(jnp.int32, (width, pairs), 1)
     ranks = lax.broadcasted_iota(jnp.int32, (2 * K * CAP, pairs), 0) // CAP % K
     limits = jnp.concatenate([limit_ref[...]] * (2 * K), axis=0)
     keep_ref[...] = jnp.where(ranks.astype(F32) < limits, 1.0, 0.0)
 
     def body(i, acc):
         acc = list(acc)
-        for j in range(BLOCK):
-            at_freq = i * (BLOCK // 2) + j // 2
-            fac_ref = own_ref if j % 2 == 0 else other_ref
-            vis = vis_ref[2 * at_freq + (core if j % 2 == 0 else 1 - core)].astype(F32)
-            swapped = pltpu.roll(vis, CAP, 0)
-            vis_re = jnp.where(top[0], vis, swapped)
-            vis_im = jnp.where(top[0], swapped, vis)
-            here = lanes == i * BLOCK + j
-            for pair in range(K // 2):
-                fac_re = fac_ref[at_freq, pl.ds(pair * 8, 8)].astype(F32)
-                fac_im = fac_ref[at_freq, pl.ds(16 + pair * 8, 8)].astype(F32)
-                re = jnp.sum(fac_re * vis_re + fac_im * vis_im, axis=1, keepdims=True)
-                im = jnp.sum(fac_re * vis_im - fac_im * vis_re, axis=1, keepdims=True)
-                acc[pair] = jnp.where(here, re, acc[pair])
-                acc[2 + pair] = jnp.where(here, im, acc[2 + pair])
+        for j in range(BLOCK // 2):
+            freq = i * (BLOCK // 2) + j
+            vis = [vis_ref[freq, part].astype(F32) for part in range(2)]
+            swapped = [pltpu.roll(v, CAP, 0) for v in vis]
+            for side, fac_ref in enumerate((own_ref, other_ref)):
+                first, second = (vis, swapped) if side == 0 else (swapped, vis)
+                vis_re = jnp.where(mine, first[0], second[0])
+                vis_im = jnp.where(mine, first[1], second[1])
+                here = lanes == 2 * freq + side
+                for pair in range(K // 2):
+                    fac_re = fac_ref[freq, pl.ds(pair * 8, 8)].astype(F32)
+                    fac_im = fac_ref[freq, pl.ds(16 + pair * 8, 8)].astype(F32)
+                    re = jnp.sum(fac_re * vis_re + fac_im * vis_im, axis=1, keepdims=True)
+                    im = jnp.sum(fac_re * vis_im - fac_im * vis_re, axis=1, keepdims=True)
+                    acc[pair] = jnp.where(here, re, acc[pair])
+                    acc[2 + pair] = jnp.where(here, im, acc[2 + pair])
         return tuple(acc)
 
-    zero = jnp.zeros((2 * CAP, pairs), F32)
+    zero = jnp.zeros((width, pairs), F32)
     acc = lax.fori_loop(0, pairs // BLOCK, body, (zero,) * 4)
     for at in range(4):
         for copy in range(out_ref.shape[0]):
@@ -134,43 +145,47 @@
 
 def synth_kernel(core_ref, part_ref, keep_ref, own_ref, other_ref, out_ref):
     core = core_ref[0]
-    pairs, _, base = out_ref.shape
+    chips, _, width, base = out_ref.shape
+    pairs = 2 * chips
     total = part_ref[0]
     for source in range(1, part_ref.shape[0]):
         total = total + part_ref[source]
     kept = jnp.where(keep_ref[...] > 0, total, 0.0).astype(BF16).astype(F32)
     kept = kept * math.sqrt(NB / K)
-    top = lax.broadcasted_iota(jnp.int32, (2 * CAP, base), 0) < CAP
+    mine = lax.broadcasted_iota(jnp.int32, (width, base), 0) // CAP == core
 
     def body(i, kept):
-        for j in range(BLOCK):
-            at_freq = i * (BLOCK // 2) + j // 2
-            fac_ref = own_ref if j % 2 == 0 else other_ref
-            re = jnp.zeros((2 * CAP, base), F32)
-            im = jnp.zeros((2 * CAP, base), F32)
-            for pair in range(K // 2):
-                fac_re = fac_ref[at_freq, pl.ds(pair * 8, 8)].astype(F32)
-                fac_im = fac_ref[at_freq, pl.ds(16 + pair * 8, 8)].astype(F32)
-                kept_re = kept[pair * 8 : pair * 8 + 8, j : j + 1]
-                kept_im = kept[16 + pair * 8 : 24 + pair * 8, j : j + 1]
-                re = re + (fac_re * kept_re - fac_im * kept_im)
-                im = im + (fac_re * kept_im + fac_im * kept_re)
-            re = re + pltpu.roll(re, CAP, 0)
-            im = im + pltpu.roll(im, CAP, 0)
-            filtered = jnp.where(top, re, im).astype(BF16)
-            out_ref[2 * at_freq + (core if j % 2 == 0 else 1 - core)] = filtered
+        for j in range(BLOCK // 2):
+            freq = i * (BLOCK // 2) + j
+            sums = []
+            for side, fac_ref in enumerate((own_ref, other_ref)):
+                re = jnp.zeros((width, base), F32)
+                im = jnp.zeros((width, base), F32)
+                lane = 2 * j + side
+                for pair in range(K // 2):
+                    fac_re = fac_ref[freq, pl.ds(pair * 8, 8)].astype(F32)
+                    fac_im = fac_ref[freq, pl.ds(16 + pair * 8, 8)].astype(F32)
+                    kept_re = kept[pair * 8 : pair * 8 + 8, lane : lane + 1]
+                    kept_im = kept[16 + pair * 8 : 24 + pair * 8, lane : lane + 1]
+                    re = re + (fac_re * kept_re - fac_im * kept_im)
+                    im = im + (fac_re * kept_im + fac_im * kept_re)
+                sums.append((re + pltpu.roll(re, CAP, 0), im + pltpu.roll(im, CAP, 0)))
+            for part in range(2):
+                out_ref[freq, part] = jnp.where(mine, sums[0][part], sums[1][part]).astype(BF16)
         return pltpu.roll(kept, pairs - BLOCK, 1)
 
     lax.fori_loop(0, pairs // BLOCK, body, kept)
 
 
 def final_kernel(target_ref, slots_ref, out_hbm, out_ref, sems):
-    rows = lax.broadcasted_iota(jnp.int32, (slots_ref.shape[0], MM), 0)
+    chips, _, width, base = slots_ref.shape
+    rows = lax.broadcasted_iota(jnp.int32, (chips * width, MM), 0)
+    placing = jnp.where(rows == target_ref[...], 1.0, 0.0).astype(BF16)
     copies = []
     for part in range(2):
-        placing = jnp.where(rows == target_ref[...] + part * CAP, 1.0, 0.0).astype(BF16)
+        slots = slots_ref[:, part].reshape(chips * width, base)
         out_ref[part] = lax.dot_general(
-            slots_ref[...], placing, (((0,), (0,)), ((), ())), preferred_element_type=F32
+            slots, placing, (((0,), (0,)), ((), ())), preferred_element_type=F32
         ).astype(BF16)
         copies.append(pltpu.make_async_copy(out_ref.at[part], out_hbm.at[part], sems.at[part]))
         copies[part].start()
@@ -188,34 +203,34 @@
     owner_row = owner.reshape(1, MM)
     width = 2 * CAP
     hbm = pl.BlockSpec(memory_space=pltpu.HBM)
+    vmem = pl.BlockSpec(memory_space=pltpu.VMEM)
+    smem = pl.BlockSpec(memory_space=pltpu.SMEM)
     wave = jnp.asarray(wave_half())
     outgoing, target = pl.pallas_call(
         dft_kernel,
         in_specs=[hbm, hbm, hbm],
+        out_specs=[hbm, vmem],
         out_shape=[
-            jax.ShapeDtypeStruct((n_freq * width, base), BF16),
+            jax.ShapeDtypeStruct((n_chip, 2, width, base), BF16),
             jax.ShapeDtypeStruct((1, MM), jnp.int32),
         ],
         scratch_shapes=[
             pltpu.VMEM((1, MM), jnp.int32),
             pltpu.VMEM((4, 2 * base, CHUNK), BF16),
             pltpu.VMEM((2, CHUNK, 2 * MM), BF16),
-            pltpu.SemaphoreType.DMA((7,)),
+            pltpu.VMEM((n_chip, 2, width, base), BF16),
+            pltpu.SemaphoreType.DMA((9,)),
         ],
         compiler_params=pltpu.CompilerParams(vmem_limit_bytes=24 << 20),
         name="dft",
     )(*(pltpu.with_memory_space_constraint(a, pltpu.HBM) for a in (owner_row, flat, wave)))
     def exchange(rows):
-        return lax.all_to_all(
-            rows.reshape(n_chip, 2 * width, base), "chip", split_axis=0, concat_axis=0, tiled=True
-        ).reshape(n_freq, width, base)
+        return lax.all_to_all(rows, "chip", split_axis=0, concat_axis=0, tiled=True)
 
     incoming = exchange(outgoing)
 
     factors, _ = lax.optimization_barrier((factors, outgoing))
     core_word = core.reshape(1)
-    smem = pl.BlockSpec(memory_space=pltpu.SMEM)
-    vmem = pl.BlockSpec(memory_space=pltpu.VMEM)
     own, sent = pl.pallas_call(
         relay_kernel,
         grid=(4,),
@@ -229,7 +244,7 @@
     other = lax.ppermute(sent, "core", [(0, 1), (1, 0)])
 
     side = jnp.arange(2, dtype=jnp.int32)[:, None]
-    slot_rows = (2 * chip + (core ^ side)) * width + jnp.arange(CAP, dtype=jnp.int32)
+    slot_rows = (2 * chip + (core ^ side)) * CAP + jnp.arange(CAP, dtype=jnp.int32)
     mine = (target == slot_rows.reshape(2 * CAP, 1)).astype(BF16)
     limits = jnp.dot(mine, counts.astype(BF16), preferred_element_type=F32)
     lane = jnp.arange(n_freq, dtype=jnp.int32)
@@ -251,7 +266,7 @@
     synthesis = pl.pallas_call(
         synth_kernel,
         in_specs=[smem, vmem, vmem, vmem, vmem],
-        out_shape=jax.ShapeDtypeStruct((n_freq, width, base), BF16),
+        out_shape=jax.ShapeDtypeStruct((n_chip, 2, width, base), BF16),
         compiler_params=pltpu.CompilerParams(vmem_limit_bytes=8 << 20),
         name="synth",
     )(core_word, partials, keep, own, other)
@@ -263,7 +278,7 @@
         scratch_shapes=[pltpu.VMEM((2, base, MM), BF16), pltpu.SemaphoreType.DMA((2,))],
         compiler_params=pltpu.CompilerParams(vmem_limit_bytes=16 << 20),
         name="final",
-    )(target, returned.reshape(n_freq * width, base))
+    )(target, returned)
     return filtered[None]
 
 

time: 106 us -> 105 us (level)
  no operation moved by 1% of the time
where the time goes in v5:
time: 105 us
  blocking collectives  45.8 us (44%)
  waiting for transfers between devices  24.9 us (24%)
  starting transfers between devices  20.8 us (20%)
  Pallas kernels  12.8 us (12%)
    all_to_all x1, blocking collectives, exchange(): return lax.all_to_all(rows, 'chip', split_axis=0, concat_axis=0, tiled=True)  35.9 us
    all_to_all x1, waiting for transfers between devices, exchange(): return lax.all_to_all(rows, 'chip', split_axis=0, concat_axis=0, tiled=True)  22.6 us
    all_to_all x1, starting transfers between devices, exchange(): return lax.all_to_all(rows, 'chip', split_axis=0, concat_axis=0, tiled=True)  18.9 us
    all_to_all x1, blocking collectives, local(): lax.all_to_all(partial, 'bl', split_axis=0, concat_axis=0, tiled=True)  9.89 us
    pallas_call x1, Pallas kernels, local(): pl.pallas_call(dft_kernel, in_specs=[hbm, hbm, hbm], out_specs=[hbm, vmem...  5.02 us
    pallas_call x1, Pallas kernels, local(): pl.pallas_call(relay_kernel, grid=(4,), in_specs=[smem, pl.BlockSpec((CAP...  4.3 us
    ppermute x1, waiting for transfers between devices, local(): other = lax.ppermute(sent, 'core', [(0, 1), (1, 0)])  2.31 us
  transfers between devices with their start and end apart: 2, of which 2 were waited for; matrix products, arithmetic and copies ran while one was open for 0% of the time, Pallas kernels for 4%

profile of v5, /device:TPU:6, one launch (start us, length us, event | category | flops | bytes accessed | tf_op | source)
XLA Modules:
  0.0 104.9 jit_solution(6675742201420309848)
XLA Ops:
  0.0 5.0 %dft.1 = (bf16[64,2,8,256]{3,2,1,0:T(8,128)(2,1)}, s32[1,384]{1,0:T(1,128)S(1)}) custom-call(s32[1,384]{1,0:T(1,128)} %bitcast.5, bf16[512,2048]{1,0:T(8,128)(2,1)} %bitcast.4, bf16[1024,768]{1,0:T(8,128)(2,1)} %constant.24.clone.wave_hbm), custom_call_target="tpu_custom_call" | custom-call | tf_op jit(solution)/shard_map/dft/pallas_call | solution.py:209
  5.0 0.0 copy-start
  5.0 18.9 %all-to-all-start = ((bf16[64,2,8,256]{3,2,1,0:T(8,128)(2,1)}), bf16[64,2,8,256]{3,2,1,0:T(8,128)(2,1)S(1)}, u32[]{:S(2)}, u32[]{:S(2)}) async-start(bf16[64,2,8,256]{3,2,1,0:T(8,128)(2,1)} %get-tuple-element.13), calls=%async_computation | async-start | bytes 1048576 | tf_op jit(solution)/shard_map/all_to_all | solution.py:228
  24.0 4.3 %relay.1 = (bf16[64,32,256]{2,1,0:T(8,128)(2,1)S(1)}, bf16[64,32,256]{2,1,0:T(8,128)(2,1)}) custom-call(s32[1]{0:T(128)} %bitcast.2.core_ref, bf16[4,128,2,4,256]{4,3,2,1,0:T(4,128)(2,1)} %fac_ref), custom_call_target="tpu_custom_call" | custom-call | tf_op jit(solution)/shard_map/relay/pallas_call | solution.py:234
  28.3 1.9 %collective-permute-start = (bf16[64,32,256]{2,1,0:T(8,128)(2,1)}, bf16[64,32,256]{2,1,0:T(8,128)(2,1)S(1)}, u32[]{:S(2)}, u32[]{:S(2)}) collective-permute-start(bf16[64,32,256]{2,1,0:T(8,128)(2,1)} %get-tuple-element.16), channel_id=1, source_target_pairs={{0,4},{4,0},{1,5},{5,1},{2,6},{6,2},{3,7},{7,3},{8,12},{12,8},{9,1... | collective-permute-start | bytes 3145736 | tf_op jit(solution)/shard_map/ppermute | solution.py:244
  30.2 0.1 iota_add_fusion
  30.3 0.1 add.46
  30.4 0.0 copy-done
  30.4 0.3 fusion
  30.7 2.3 %collective-permute-done.other_ref = bf16[64,32,256]{2,1,0:T(8,128)(2,1)S(1)} collective-permute-done((bf16[64,32,256]{2,1,0:T(8,128)(2,1)}, bf16[64,32,256]{2,1,0:T(8,128)(2,1)S(1)}, u32[]{:S(2)}, u32[]{:S(2)}) %collective-permute-start) | collective-permute-done | bytes 1048608 | tf_op jit(solution)/shard_map/ppermute | solution.py:244
  33.0 22.6 %all-to-all-done.vis_ref = bf16[64,2,8,256]{3,2,1,0:T(8,128)(2,1)S(1)} async-done(((bf16[64,2,8,256]{3,2,1,0:T(8,128)(2,1)}), bf16[64,2,8,256]{3,2,1,0:T(8,128)(2,1)S(1)}, u32[]{:S(2)}, u32[]{:S(2)}) %all-to-all-start) | async-done | bytes 524320 | tf_op jit(solution)/shard_map/all_to_all | solution.py:228
  55.6 1.1 %coef.1 = (f32[4,32,128]{2,1,0:T(8,128)S(1)}, f32[32,128]{1,0:T(8,128)S(1)}) custom-call(s32[1]{0:T(128)} %bitcast.2.core_ref, bf16[64,2,8,256]{3,2,1,0:T(8,128)(2,1)S(1)} %all-to-all-done.vis_ref, bf16[64,32,256]{2,1,0:T(8,128)(2,1)S(1)} %get-tuple-element.15.own_ref, bf16[64,32,256]{2,1,0:T(8,128)(2,1)S(1)} %collective-permute-done.other_ref, ...), custom_call_target="tpu_custom_call" | custom-call | tf_op jit(solution)/shard_map/coef/pallas_call | solution.py:255
  56.8 9.9 %all_to_all.15.part_ref = f32[4,32,128]{2,1,0:T(8,128)S(1)} all-to-all(f32[4,32,128]{2,1,0:T(8,128)S(1)} %get-tuple-element.17), channel_id=1, replica_groups=mesh['chip'=64,'core'=2,'bl'=4] {'bl'}, dimensions={0} | all-to-all | bytes 131072 | tf_op jit(solution)/shard_map/all_to_all | solution.py:265
  66.6 1.2 %synth.1 = bf16[64,2,8,256]{3,2,1,0:T(8,128)(2,1)S(1)} custom-call(s32[1]{0:T(128)} %bitcast.2.core_ref, f32[4,32,128]{2,1,0:T(8,128)S(1)} %all_to_all.15.part_ref, f32[32,128]{1,0:T(8,128)S(1)} %get-tuple-element.18.keep_ref, bf16[64,32,256]{2,1,0:T(8,128)(2,1)S(1)} %get-tuple-element.15.own_ref, bf16[64,32,256]{2,1,0:T(8,128)(2,1)S(1)} %collective-permute-done.other_ref), custom_call_target="tpu_custom_call" | custom-call | tf_op jit(solution)/shard_map/synth/pallas_call | solution.py:266
  67.8 35.9 %all_to_all.16.slots_ref = bf16[64,2,8,256]{3,2,1,0:T(8,128)(2,1)S(1)} all-to-all(bf16[64,2,8,256]{3,2,1,0:T(8,128)(2,1)S(1)} %synth.1), channel_id=1, replica_groups=mesh['chip'=64,'core'=2,'bl'=4] {'chip'}, dimensions={0} | all-to-all | bytes 1048576 | tf_op jit(solution)/shard_map/all_to_all | solution.py:228
  103.8 1.2 %final.1 = bf16[2,256,384]{2,1,0:T(8,128)(2,1)} custom-call(s32[1,384]{1,0:T(1,128)S(1)} %get-tuple-element.12.target_ref, bf16[64,2,8,256]{3,2,1,0:T(8,128)(2,1)S(1)} %all_to_all.16.slots_ref), custom_call_target="tpu_custom_call" | custom-call | tf_op jit(solution)/shard_map/final/pallas_call | solution.py:274
  (5 shorter events, 0.0 us)
Async XLA Ops:
  5.0 25.4 %copy-start = (s32[384,128]{1,0:T(8,128)S(1)}, s32[384,128]{1,0:T(8,128)}, u32[]{:S(2)}) copy-start(s32[384,128]{1,0:T(8,128)} %param.7) | copy-start | bytes 589828
  5.0 50.6 %all-to-all-start = ((bf16[64,2,8,256]{3,2,1,0:T(8,128)(2,1)}), bf16[64,2,8,256]{3,2,1,0:T(8,128)(2,1)S(1)}, u32[]{:S(2)}, u32[]{:S(2)}) async-start(bf16[64,2,8,256]{3,2,1,0:T(8,128)(2,1)} %get-tuple-element.13), calls=%async_computation | async-start | bytes 1048576 | tf_op jit(solution)/shard_map/all_to_all | solution.py:228
  28.3 4.8 %collective-permute-start = (bf16[64,32,256]{2,1,0:T(8,128)(2,1)}, bf16[64,32,256]{2,1,0:T(8,128)(2,1)S(1)}, u32[]{:S(2)}, u32[]{:S(2)}) collective-permute-start(bf16[64,32,256]{2,1,0:T(8,128)(2,1)} %get-tuple-element.16), channel_id=1, source_target_pairs={{0,4},{4,0},{1,5},{5,1},{2,6},{6,2},{3,7},{7,3},{8,12},{12,8},{9,1... | collective-permute-start | bytes 3145736 | tf_op jit(solution)/shard_map/ppermute | solution.py:244

commit v6 on v5

--- a/solution.py
+++ b/solution.py
@@ -14,7 +14,7 @@
 MM = 384
 CAP = 4
 CHUNK = NT // 4
-BLOCK = 32
+BLOCK = 64
 F32 = jnp.float32
 BF16 = jnp.bfloat16
 
@@ -100,7 +100,7 @@
                         rows = fac_ref[slot, 2 * i + side, part, :, pl.ds(lane * 128, 128)]
                         first = part * K * CAP + slot
                         rows_ref[lane, pl.ds(first, K, stride=CAP), :] = rows.astype(F32)
-                out_ref[i, :, pl.ds(lane * 128, 128)] = rows_ref[lane].astype(BF16)
+                out_ref[i, :, pl.ds(lane * 128, 128)] = rows_ref[lane, : out_ref.shape[1]].astype(BF16)
         return carry
 
     lax.fori_loop(0, own_ref.shape[0], body, 0, unroll=4)
@@ -237,7 +237,7 @@
         in_specs=[smem, pl.BlockSpec((CAP, n_freq // 4, 2, K, base), lambda i: (0, i, 0, 0, 0))],
         out_specs=[pl.BlockSpec((n_chip // 4, 2 * K * CAP, base), lambda i: (i, 0, 0))] * 2,
         out_shape=[jax.ShapeDtypeStruct((n_chip, 2 * K * CAP, base), BF16)] * 2,
-        scratch_shapes=[pltpu.VMEM((base // 128, 2 * K * CAP, 128), F32)],
+        scratch_shapes=[pltpu.VMEM((base // 128, 2 * K * CAP + 8, 128), F32)],
         compiler_params=pltpu.CompilerParams(vmem_limit_bytes=8 << 20),
         name="relay",
     )(core_word, pltpu.with_memory_space_constraint(factors, pltpu.HBM))

time: 105 us -> 105 us (level)
  no operation moved by 1% of the time
where the time goes in v6:
time: 105 us
  blocking collectives  45.8 us (44%)
  waiting for transfers between devices  24.9 us (24%)
  starting transfers between devices  20.8 us (20%)
  Pallas kernels  12.5 us (12%)
    all_to_all x1, blocking collectives, exchange(): return lax.all_to_all(rows, 'chip', split_axis=0, concat_axis=0, tiled=True)  35.9 us
    all_to_all x1, waiting for transfers between devices, exchange(): return lax.all_to_all(rows, 'chip', split_axis=0, concat_axis=0, tiled=True)  22.6 us
    all_to_all x1, starting transfers between devices, exchange(): return lax.all_to_all(rows, 'chip', split_axis=0, concat_axis=0, tiled=True)  18.9 us
    all_to_all x1, blocking collectives, local(): lax.all_to_all(partial, 'bl', split_axis=0, concat_axis=0, tiled=True)  9.89 us
    pallas_call x1, Pallas kernels, local(): pl.pallas_call(dft_kernel, in_specs=[hbm, hbm, hbm], out_specs=[hbm, vmem...  5.02 us
    pallas_call x1, Pallas kernels, local(): pl.pallas_call(relay_kernel, grid=(4,), in_specs=[smem, pl.BlockSpec((CAP...  4.31 us
    ppermute x1, waiting for transfers between devices, local(): other = lax.ppermute(sent, 'core', [(0, 1), (1, 0)])  2.31 us
  transfers between devices with their start and end apart: 2, of which 2 were waited for; matrix products, arithmetic and copies ran while one was open for 0% of the time, Pallas kernels for 4%

profile of v6, /device:TPU:6, one launch (start us, length us, event | category | flops | bytes accessed | tf_op | source)
XLA Modules:
  0.0 104.6 jit_solution(833237445563835853)
XLA Ops:
  0.0 5.0 %dft.1 = (bf16[64,2,8,256]{3,2,1,0:T(8,128)(2,1)}, s32[1,384]{1,0:T(1,128)S(1)}) custom-call(s32[1,384]{1,0:T(1,128)} %bitcast.5, bf16[512,2048]{1,0:T(8,128)(2,1)} %bitcast.4, bf16[1024,768]{1,0:T(8,128)(2,1)} %constant.24.clone.wave_hbm), custom_call_target="tpu_custom_call" | custom-call | tf_op jit(solution)/shard_map/dft/pallas_call | solution.py:209
  5.0 0.0 copy-start
  5.0 18.9 %all-to-all-start = ((bf16[64,2,8,256]{3,2,1,0:T(8,128)(2,1)}), bf16[64,2,8,256]{3,2,1,0:T(8,128)(2,1)S(1)}, u32[]{:S(2)}, u32[]{:S(2)}) async-start(bf16[64,2,8,256]{3,2,1,0:T(8,128)(2,1)} %get-tuple-element.13), calls=%async_computation | async-start | bytes 1048576 | tf_op jit(solution)/shard_map/all_to_all | solution.py:228
  24.0 4.3 %relay.1 = (bf16[64,32,256]{2,1,0:T(8,128)(2,1)S(1)}, bf16[64,32,256]{2,1,0:T(8,128)(2,1)}) custom-call(s32[1]{0:T(128)} %bitcast.2.core_ref, bf16[4,128,2,4,256]{4,3,2,1,0:T(4,128)(2,1)} %fac_ref), custom_call_target="tpu_custom_call" | custom-call | tf_op jit(solution)/shard_map/relay/pallas_call | solution.py:234
  28.3 1.9 %collective-permute-start = (bf16[64,32,256]{2,1,0:T(8,128)(2,1)}, bf16[64,32,256]{2,1,0:T(8,128)(2,1)S(1)}, u32[]{:S(2)}, u32[]{:S(2)}) collective-permute-start(bf16[64,32,256]{2,1,0:T(8,128)(2,1)} %get-tuple-element.16), channel_id=1, source_target_pairs={{0,4},{4,0},{1,5},{5,1},{2,6},{6,2},{3,7},{7,3},{8,12},{12,8},{9,1... | collective-permute-start | bytes 3145736 | tf_op jit(solution)/shard_map/ppermute | solution.py:244
  30.2 0.1 iota_add_fusion
  30.3 0.1 add.46
  30.4 0.0 copy-done
  30.4 0.3 fusion
  30.7 2.3 %collective-permute-done.other_ref = bf16[64,32,256]{2,1,0:T(8,128)(2,1)S(1)} collective-permute-done((bf16[64,32,256]{2,1,0:T(8,128)(2,1)}, bf16[64,32,256]{2,1,0:T(8,128)(2,1)S(1)}, u32[]{:S(2)}, u32[]{:S(2)}) %collective-permute-start) | collective-permute-done | bytes 1048608 | tf_op jit(solution)/shard_map/ppermute | solution.py:244
  33.0 22.6 %all-to-all-done.vis_ref = bf16[64,2,8,256]{3,2,1,0:T(8,128)(2,1)S(1)} async-done(((bf16[64,2,8,256]{3,2,1,0:T(8,128)(2,1)}), bf16[64,2,8,256]{3,2,1,0:T(8,128)(2,1)S(1)}, u32[]{:S(2)}, u32[]{:S(2)}) %all-to-all-start) | async-done | bytes 524320 | tf_op jit(solution)/shard_map/all_to_all | solution.py:228
  55.6 1.0 coef.1
  56.6 9.9 %all_to_all.15.part_ref = f32[4,32,128]{2,1,0:T(8,128)S(1)} all-to-all(f32[4,32,128]{2,1,0:T(8,128)S(1)} %get-tuple-element.17), channel_id=1, replica_groups=mesh['chip'=64,'core'=2,'bl'=4] {'bl'}, dimensions={0} | all-to-all | bytes 131072 | tf_op jit(solution)/shard_map/all_to_all | solution.py:265
  66.5 1.0 synth.1
  67.5 35.9 %all_to_all.16.slots_ref = bf16[64,2,8,256]{3,2,1,0:T(8,128)(2,1)S(1)} all-to-all(bf16[64,2,8,256]{3,2,1,0:T(8,128)(2,1)S(1)} %synth.1), channel_id=1, replica_groups=mesh['chip'=64,'core'=2,'bl'=4] {'chip'}, dimensions={0} | all-to-all | bytes 1048576 | tf_op jit(solution)/shard_map/all_to_all | solution.py:228
  103.5 1.2 %final.1 = bf16[2,256,384]{2,1,0:T(8,128)(2,1)} custom-call(s32[1,384]{1,0:T(1,128)S(1)} %get-tuple-element.12.target_ref, bf16[64,2,8,256]{3,2,1,0:T(8,128)(2,1)S(1)} %all_to_all.16.slots_ref), custom_call_target="tpu_custom_call" | custom-call | tf_op jit(solution)/shard_map/final/pallas_call | solution.py:274
  (5 shorter events, 0.0 us)
Async XLA Ops:
  5.0 25.4 %copy-start = (s32[384,128]{1,0:T(8,128)S(1)}, s32[384,128]{1,0:T(8,128)}, u32[]{:S(2)}) copy-start(s32[384,128]{1,0:T(8,128)} %param.7) | copy-start | bytes 589828
  5.0 50.6 %all-to-all-start = ((bf16[64,2,8,256]{3,2,1,0:T(8,128)(2,1)}), bf16[64,2,8,256]{3,2,1,0:T(8,128)(2,1)S(1)}, u32[]{:S(2)}, u32[]{:S(2)}) async-start(bf16[64,2,8,256]{3,2,1,0:T(8,128)(2,1)} %get-tuple-element.13), calls=%async_computation | async-start | bytes 1048576 | tf_op jit(solution)/shard_map/all_to_all | solution.py:228
  28.3 4.8 %collective-permute-start = (bf16[64,32,256]{2,1,0:T(8,128)(2,1)}, bf16[64,32,256]{2,1,0:T(8,128)(2,1)S(1)}, u32[]{:S(2)}, u32[]{:S(2)}) collective-permute-start(bf16[64,32,256]{2,1,0:T(8,128)(2,1)} %get-tuple-element.16), channel_id=1, source_target_pairs={{0,4},{4,0},{1,5},{5,1},{2,6},{6,2},{3,7},{7,3},{8,12},{12,8},{9,1... | collective-permute-start | bytes 3145736 | tf_op jit(solution)/shard_map/ppermute | solution.py:244

commit v7 on v6

--- a/solution.py
+++ b/solution.py
@@ -14,7 +14,7 @@
 MM = 384
 CAP = 4
 CHUNK = NT // 4
-BLOCK = 64
+BLOCK = 128
 F32 = jnp.float32
 BF16 = jnp.bfloat16
 

time: 105 us -> 105 us (level)
  no operation moved by 1% of the time
where the time goes in v7:
time: 105 us; the launch traced here: 104 us
  blocking collectives  45.8 us (44%)
  waiting for transfers between devices  24.9 us (24%)
  starting transfers between devices  20.8 us (20%)
  Pallas kernels  12.3 us (12%)
    all_to_all x1, blocking collectives, exchange(): return lax.all_to_all(rows, 'chip', split_axis=0, concat_axis=0, tiled=True)  35.9 us
    all_to_all x1, waiting for transfers between devices, exchange(): return lax.all_to_all(rows, 'chip', split_axis=0, concat_axis=0, tiled=True)  22.6 us
    all_to_all x1, starting transfers between devices, exchange(): return lax.all_to_all(rows, 'chip', split_axis=0, concat_axis=0, tiled=True)  18.9 us
    all_to_all x1, blocking collectives, local(): lax.all_to_all(partial, 'bl', split_axis=0, concat_axis=0, tiled=True)  9.89 us
    pallas_call x1, Pallas kernels, local(): pl.pallas_call(dft_kernel, in_specs=[hbm, hbm, hbm], out_specs=[hbm, vmem...  5.02 us
    pallas_call x1, Pallas kernels, local(): pl.pallas_call(relay_kernel, grid=(4,), in_specs=[smem, pl.BlockSpec((CAP...  4.31 us
    ppermute x1, waiting for transfers between devices, local(): other = lax.ppermute(sent, 'core', [(0, 1), (1, 0)])  2.31 us
  transfers between devices with their start and end apart: 2, of which 2 were waited for; matrix products, arithmetic and copies ran while one was open for 0% of the time, Pallas kernels for 4%

profile of v7, /device:TPU:6, one launch (start us, length us, event | category | flops | bytes accessed | tf_op | source)
XLA Modules:
  0.0 104.5 jit_solution(10219199589056299739)
XLA Ops:
  0.0 5.0 %dft.1 = (bf16[64,2,8,256]{3,2,1,0:T(8,128)(2,1)}, s32[1,384]{1,0:T(1,128)S(1)}) custom-call(s32[1,384]{1,0:T(1,128)} %bitcast.5, bf16[512,2048]{1,0:T(8,128)(2,1)} %bitcast.4, bf16[1024,768]{1,0:T(8,128)(2,1)} %constant.24.clone.wave_hbm), custom_call_target="tpu_custom_call" | custom-call | tf_op jit(solution)/shard_map/dft/pallas_call | solution.py:209
  5.0 0.0 copy-start
  5.0 18.9 %all-to-all-start = ((bf16[64,2,8,256]{3,2,1,0:T(8,128)(2,1)}), bf16[64,2,8,256]{3,2,1,0:T(8,128)(2,1)S(1)}, u32[]{:S(2)}, u32[]{:S(2)}) async-start(bf16[64,2,8,256]{3,2,1,0:T(8,128)(2,1)} %get-tuple-element.13), calls=%async_computation | async-start | bytes 1048576 | tf_op jit(solution)/shard_map/all_to_all | solution.py:228
  24.0 4.3 %relay.1 = (bf16[64,32,256]{2,1,0:T(8,128)(2,1)S(1)}, bf16[64,32,256]{2,1,0:T(8,128)(2,1)}) custom-call(s32[1]{0:T(128)} %bitcast.2.core_ref, bf16[4,128,2,4,256]{4,3,2,1,0:T(4,128)(2,1)} %fac_ref), custom_call_target="tpu_custom_call" | custom-call | tf_op jit(solution)/shard_map/relay/pallas_call | solution.py:234
  28.3 1.9 %collective-permute-start = (bf16[64,32,256]{2,1,0:T(8,128)(2,1)}, bf16[64,32,256]{2,1,0:T(8,128)(2,1)S(1)}, u32[]{:S(2)}, u32[]{:S(2)}) collective-permute-start(bf16[64,32,256]{2,1,0:T(8,128)(2,1)} %get-tuple-element.16), channel_id=1, source_target_pairs={{0,4},{4,0},{1,5},{5,1},{2,6},{6,2},{3,7},{7,3},{8,12},{12,8},{9,1... | collective-permute-start | bytes 3145736 | tf_op jit(solution)/shard_map/ppermute | solution.py:244
  30.2 0.1 iota_add_fusion
  30.3 0.1 add.46
  30.4 0.0 copy-done
  30.4 0.3 fusion
  30.7 2.3 %collective-permute-done.other_ref = bf16[64,32,256]{2,1,0:T(8,128)(2,1)S(1)} collective-permute-done((bf16[64,32,256]{2,1,0:T(8,128)(2,1)}, bf16[64,32,256]{2,1,0:T(8,128)(2,1)S(1)}, u32[]{:S(2)}, u32[]{:S(2)}) %collective-permute-start) | collective-permute-done | bytes 1048608 | tf_op jit(solution)/shard_map/ppermute | solution.py:244
  33.0 22.6 %all-to-all-done.vis_ref = bf16[64,2,8,256]{3,2,1,0:T(8,128)(2,1)S(1)} async-done(((bf16[64,2,8,256]{3,2,1,0:T(8,128)(2,1)}), bf16[64,2,8,256]{3,2,1,0:T(8,128)(2,1)S(1)}, u32[]{:S(2)}, u32[]{:S(2)}) %all-to-all-start) | async-done | bytes 524320 | tf_op jit(solution)/shard_map/all_to_all | solution.py:228
  55.6 0.9 coef.1
  56.5 9.9 %all_to_all.15.part_ref = f32[4,32,128]{2,1,0:T(8,128)S(1)} all-to-all(f32[4,32,128]{2,1,0:T(8,128)S(1)} %get-tuple-element.17), channel_id=1, replica_groups=mesh['chip'=64,'core'=2,'bl'=4] {'bl'}, dimensions={0} | all-to-all | bytes 131072 | tf_op jit(solution)/shard_map/all_to_all | solution.py:265
  66.4 0.9 synth.1
  67.3 35.9 %all_to_all.16.slots_ref = bf16[64,2,8,256]{3,2,1,0:T(8,128)(2,1)S(1)} all-to-all(bf16[64,2,8,256]{3,2,1,0:T(8,128)(2,1)S(1)} %synth.1), channel_id=1, replica_groups=mesh['chip'=64,'core'=2,'bl'=4] {'chip'}, dimensions={0} | all-to-all | bytes 1048576 | tf_op jit(solution)/shard_map/all_to_all | solution.py:228
  103.3 1.2 %final.1 = bf16[2,256,384]{2,1,0:T(8,128)(2,1)} custom-call(s32[1,384]{1,0:T(1,128)S(1)} %get-tuple-element.12.target_ref, bf16[64,2,8,256]{3,2,1,0:T(8,128)(2,1)S(1)} %all_to_all.16.slots_ref), custom_call_target="tpu_custom_call" | custom-call | tf_op jit(solution)/shard_map/final/pallas_call | solution.py:274
  (5 shorter events, 0.0 us)
Async XLA Ops:
  5.0 25.4 %copy-start = (s32[384,128]{1,0:T(8,128)S(1)}, s32[384,128]{1,0:T(8,128)}, u32[]{:S(2)}) copy-start(s32[384,128]{1,0:T(8,128)} %param.7) | copy-start | bytes 589828
  5.0 50.6 %all-to-all-start = ((bf16[64,2,8,256]{3,2,1,0:T(8,128)(2,1)}), bf16[64,2,8,256]{3,2,1,0:T(8,128)(2,1)S(1)}, u32[]{:S(2)}, u32[]{:S(2)}) async-start(bf16[64,2,8,256]{3,2,1,0:T(8,128)(2,1)} %get-tuple-element.13), calls=%async_computation | async-start | bytes 1048576 | tf_op jit(solution)/shard_map/all_to_all | solution.py:228
  28.3 4.8 %collective-permute-start = (bf16[64,32,256]{2,1,0:T(8,128)(2,1)}, bf16[64,32,256]{2,1,0:T(8,128)(2,1)S(1)}, u32[]{:S(2)}, u32[]{:S(2)}) collective-permute-start(bf16[64,32,256]{2,1,0:T(8,128)(2,1)} %get-tuple-element.16), channel_id=1, source_target_pairs={{0,4},{4,0},{1,5},{5,1},{2,6},{6,2},{3,7},{7,3},{8,12},{12,8},{9,1... | collective-permute-start | bytes 3145736 | tf_op jit(solution)/shard_map/ppermute | solution.py:244

commit v8 on v7

--- a/solution.py
+++ b/solution.py
@@ -89,8 +89,11 @@
         copy.wait()
 
 
-def relay_kernel(core_ref, fac_ref, own_ref, sent_ref, rows_ref):
+def relay_kernel(core_ref, target_ref, fac_ref, own_ref, sent_ref, placing_ref, rows_ref):
     core = core_ref[0]
+    rows = lax.broadcasted_iota(jnp.int32, placing_ref.shape, 0)
+    rows = rows + pl.program_id(0) * placing_ref.shape[0]
+    placing_ref[...] = jnp.where(rows == target_ref[...], 1.0, 0.0).astype(BF16)
 
     def body(i, carry):
         for out_ref, side in ((own_ref, core), (sent_ref, 1 - core)):
@@ -177,10 +180,9 @@
     lax.fori_loop(0, pairs // BLOCK, body, kept)
 
 
-def final_kernel(target_ref, slots_ref, out_hbm, out_ref, sems):
+def final_kernel(placing_ref, slots_ref, out_hbm, out_ref, sems):
     chips, _, width, base = slots_ref.shape
-    rows = lax.broadcasted_iota(jnp.int32, (chips * width, MM), 0)
-    placing = jnp.where(rows == target_ref[...], 1.0, 0.0).astype(BF16)
+    placing = placing_ref[...]
     copies = []
     for part in range(2):
         slots = slots_ref[:, part].reshape(chips * width, base)
@@ -231,16 +233,22 @@
 
     factors, _ = lax.optimization_barrier((factors, outgoing))
     core_word = core.reshape(1)
-    own, sent = pl.pallas_call(
+    own, sent, placing = pl.pallas_call(
         relay_kernel,
         grid=(4,),
-        in_specs=[smem, pl.BlockSpec((CAP, n_freq // 4, 2, K, base), lambda i: (0, i, 0, 0, 0))],
-        out_specs=[pl.BlockSpec((n_chip // 4, 2 * K * CAP, base), lambda i: (i, 0, 0))] * 2,
-        out_shape=[jax.ShapeDtypeStruct((n_chip, 2 * K * CAP, base), BF16)] * 2,
+        in_specs=[
+            smem,
+            pl.BlockSpec((1, MM), lambda i: (0, 0)),
+            pl.BlockSpec((CAP, n_freq // 4, 2, K, base), lambda i: (0, i, 0, 0, 0)),
+        ],
+        out_specs=[pl.BlockSpec((n_chip // 4, 2 * K * CAP, base), lambda i: (i, 0, 0))] * 2
+        + [pl.BlockSpec((n_freq * CAP // 4, MM), lambda i: (i, 0))],
+        out_shape=[jax.ShapeDtypeStruct((n_chip, 2 * K * CAP, base), BF16)] * 2
+        + [jax.ShapeDtypeStruct((n_freq * CAP, MM), BF16)],
         scratch_shapes=[pltpu.VMEM((base // 128, 2 * K * CAP + 8, 128), F32)],
         compiler_params=pltpu.CompilerParams(vmem_limit_bytes=8 << 20),
         name="relay",
-    )(core_word, pltpu.with_memory_space_constraint(factors, pltpu.HBM))
+    )(core_word, target, pltpu.with_memory_space_constraint(factors, pltpu.HBM))
     other = lax.ppermute(sent, "core", [(0, 1), (1, 0)])
 
     side = jnp.arange(2, dtype=jnp.int32)[:, None]
@@ -278,7 +286,7 @@
         scratch_shapes=[pltpu.VMEM((2, base, MM), BF16), pltpu.SemaphoreType.DMA((2,))],
         compiler_params=pltpu.CompilerParams(vmem_limit_bytes=16 << 20),
         name="final",
-    )(target, returned)
+    )(placing, returned)
     return filtered[None]
 
 

time: 105 us -> 105 us (level)
  no operation moved by 1% of the time
where the time goes in v8:
time: 105 us; the launch traced here: 104 us
  blocking collectives  45.8 us (44%)
  waiting for transfers between devices  24.9 us (24%)
  starting transfers between devices  20.8 us (20%)
  Pallas kernels  12.3 us (12%)
    all_to_all x1, blocking collectives, exchange(): return lax.all_to_all(rows, 'chip', split_axis=0, concat_axis=0, tiled=True)  35.9 us
    all_to_all x1, waiting for transfers between devices, exchange(): return lax.all_to_all(rows, 'chip', split_axis=0, concat_axis=0, tiled=True)  22.6 us
    all_to_all x1, starting transfers between devices, exchange(): return lax.all_to_all(rows, 'chip', split_axis=0, concat_axis=0, tiled=True)  18.9 us
    all_to_all x1, blocking collectives, local(): lax.all_to_all(partial, 'bl', split_axis=0, concat_axis=0, tiled=True)  9.89 us
    pallas_call x1, Pallas kernels, local(): pl.pallas_call(dft_kernel, in_specs=[hbm, hbm, hbm], out_specs=[hbm, vmem...  5.02 us
    pallas_call x1, Pallas kernels, local(): pl.pallas_call(relay_kernel, grid=(4,), in_specs=[smem, pl.BlockSpec((1,...  4.36 us
    ppermute x1, waiting for transfers between devices, local(): other = lax.ppermute(sent, 'core', [(0, 1), (1, 0)])  2.31 us
  transfers between devices with their start and end apart: 2, of which 2 were waited for; matrix products, arithmetic and copies ran while one was open for 0% of the time, Pallas kernels for 4%

profile of v8, /device:TPU:6, one launch (start us, length us, event | category | flops | bytes accessed | tf_op | source)
XLA Modules:
  0.0 104.4 jit_solution(2778161290179847613)
XLA Ops:
  0.0 5.0 %dft.1 = (bf16[64,2,8,256]{3,2,1,0:T(8,128)(2,1)}, s32[1,384]{1,0:T(1,128)S(1)}) custom-call(s32[1,384]{1,0:T(1,128)} %bitcast.5, bf16[512,2048]{1,0:T(8,128)(2,1)} %bitcast.4, bf16[1024,768]{1,0:T(8,128)(2,1)} %constant.24.clone.wave_hbm), custom_call_target="tpu_custom_call" | custom-call | tf_op jit(solution)/shard_map/dft/pallas_call | solution.py:211
  5.0 0.0 copy-start
  5.0 18.9 %all-to-all-start = ((bf16[64,2,8,256]{3,2,1,0:T(8,128)(2,1)}), bf16[64,2,8,256]{3,2,1,0:T(8,128)(2,1)S(1)}, u32[]{:S(2)}, u32[]{:S(2)}) async-start(bf16[64,2,8,256]{3,2,1,0:T(8,128)(2,1)} %get-tuple-element.14), calls=%async_computation | async-start | bytes 1048576 | tf_op jit(solution)/shard_map/all_to_all | solution.py:230
  24.0 4.4 %relay.1 = (bf16[64,32,256]{2,1,0:T(8,128)(2,1)S(1)}, bf16[64,32,256]{2,1,0:T(8,128)(2,1)}, bf16[512,384]{1,0:T(8,128)(2,1)S(1)}) custom-call(s32[1]{0:T(128)} %bitcast.core_ref, s32[1,384]{1,0:T(1,128)S(1)} %get-tuple-element.13.target_ref, bf16[4,128,2,4,256]{4,3,2,1,0:T(4,128)(2,1)} %fac_ref), custom_call_target="tpu_custom_call" | custom-call | tf_op jit(solution)/shard_map/relay/pallas_call | solution.py:236
  28.3 1.9 %collective-permute-start = (bf16[64,32,256]{2,1,0:T(8,128)(2,1)}, bf16[64,32,256]{2,1,0:T(8,128)(2,1)S(1)}, u32[]{:S(2)}, u32[]{:S(2)}) collective-permute-start(bf16[64,32,256]{2,1,0:T(8,128)(2,1)} %get-tuple-element.18), channel_id=1, source_target_pairs={{0,4},{4,0},{1,5},{5,1},{2,6},{6,2},{3,7},{7,3},{8,12},{12,8},{9,1... | collective-permute-start | bytes 3145736 | tf_op jit(solution)/shard_map/ppermute | solution.py:252
  30.3 0.1 iota_add_fusion
  30.3 0.1 add.46
  30.5 0.0 copy-done
  30.5 0.3 fusion
  30.8 2.3 %collective-permute-done.other_ref = bf16[64,32,256]{2,1,0:T(8,128)(2,1)S(1)} collective-permute-done((bf16[64,32,256]{2,1,0:T(8,128)(2,1)}, bf16[64,32,256]{2,1,0:T(8,128)(2,1)S(1)}, u32[]{:S(2)}, u32[]{:S(2)}) %collective-permute-start) | collective-permute-done | bytes 1048608 | tf_op jit(solution)/shard_map/ppermute | solution.py:252
  33.1 22.6 %all-to-all-done.vis_ref = bf16[64,2,8,256]{3,2,1,0:T(8,128)(2,1)S(1)} async-done(((bf16[64,2,8,256]{3,2,1,0:T(8,128)(2,1)}), bf16[64,2,8,256]{3,2,1,0:T(8,128)(2,1)S(1)}, u32[]{:S(2)}, u32[]{:S(2)}) %all-to-all-start) | async-done | bytes 524320 | tf_op jit(solution)/shard_map/all_to_all | solution.py:230
  55.6 0.9 coef.1
  56.5 9.9 %all_to_all.15.part_ref = f32[4,32,128]{2,1,0:T(8,128)S(1)} all-to-all(f32[4,32,128]{2,1,0:T(8,128)S(1)} %get-tuple-element.19), channel_id=1, replica_groups=mesh['chip'=64,'core'=2,'bl'=4] {'bl'}, dimensions={0} | all-to-all | bytes 131072 | tf_op jit(solution)/shard_map/all_to_all | solution.py:273
  66.4 0.9 synth.1
  67.3 35.9 %all_to_all.16.slots_ref = bf16[64,2,8,256]{3,2,1,0:T(8,128)(2,1)S(1)} all-to-all(bf16[64,2,8,256]{3,2,1,0:T(8,128)(2,1)S(1)} %synth.1), channel_id=1, replica_groups=mesh['chip'=64,'core'=2,'bl'=4] {'chip'}, dimensions={0} | all-to-all | bytes 1048576 | tf_op jit(solution)/shard_map/all_to_all | solution.py:230
  103.3 1.2 %final.1 = bf16[2,256,384]{2,1,0:T(8,128)(2,1)} custom-call(bf16[512,384]{1,0:T(8,128)(2,1)S(1)} %get-tuple-element.16.placing_ref, bf16[64,2,8,256]{3,2,1,0:T(8,128)(2,1)S(1)} %all_to_all.16.slots_ref), custom_call_target="tpu_custom_call" | custom-call | tf_op jit(solution)/shard_map/final/pallas_call | solution.py:282
  (5 shorter events, 0.0 us)
Async XLA Ops:
  5.0 25.4 %copy-start = (s32[384,128]{1,0:T(8,128)S(1)}, s32[384,128]{1,0:T(8,128)}, u32[]{:S(2)}) copy-start(s32[384,128]{1,0:T(8,128)} %param.7) | copy-start | bytes 589828
  5.0 50.6 %all-to-all-start = ((bf16[64,2,8,256]{3,2,1,0:T(8,128)(2,1)}), bf16[64,2,8,256]{3,2,1,0:T(8,128)(2,1)S(1)}, u32[]{:S(2)}, u32[]{:S(2)}) async-start(bf16[64,2,8,256]{3,2,1,0:T(8,128)(2,1)} %get-tuple-element.14), calls=%async_computation | async-start | bytes 1048576 | tf_op jit(solution)/shard_map/all_to_all | solution.py:230
  28.3 4.8 %collective-permute-start = (bf16[64,32,256]{2,1,0:T(8,128)(2,1)}, bf16[64,32,256]{2,1,0:T(8,128)(2,1)S(1)}, u32[]{:S(2)}, u32[]{:S(2)}) collective-permute-start(bf16[64,32,256]{2,1,0:T(8,128)(2,1)} %get-tuple-element.18), channel_id=1, source_target_pairs={{0,4},{4,0},{1,5},{5,1},{2,6},{6,2},{3,7},{7,3},{8,12},{12,8},{9,1... | collective-permute-start | bytes 3145736 | tf_op jit(solution)/shard_map/ppermute | solution.py:252

commit v9 on v7

--- a/solution.py
+++ b/solution.py
@@ -81,10 +81,14 @@
             placing, modes.astype(BF16), (((1,), (1,)), ((), ())), preferred_element_type=F32
         )
         out_ref[:, part] = placed.astype(BF16).reshape(chips, width, base)
-        out_copies.append(
-            pltpu.make_async_copy(out_ref.at[:, part], out_hbm.at[:, part], sems.at[7 + part])
-        )
-        out_copies[part].start()
+        for half in range(2):
+            some = pl.ds(half * (chips // 2), chips // 2)
+            out_copies.append(
+                pltpu.make_async_copy(
+                    out_ref.at[some, part], out_hbm.at[some, part], sems.at[7 + 2 * part + half]
+                )
+            )
+            out_copies[-1].start()
     for copy in out_copies:
         copy.wait()
 
@@ -219,7 +223,7 @@
             pltpu.VMEM((4, 2 * base, CHUNK), BF16),
             pltpu.VMEM((2, CHUNK, 2 * MM), BF16),
             pltpu.VMEM((n_chip, 2, width, base), BF16),
-            pltpu.SemaphoreType.DMA((9,)),
+            pltpu.SemaphoreType.DMA((11,)),
         ],
         compiler_params=pltpu.CompilerParams(vmem_limit_bytes=24 << 20),
         name="dft",

time: 105 us -> 105 us (level)
  no operation moved by 1% of the time
where the time goes in v9:
time: 105 us; the launch traced here: 104 us
  blocking collectives  45.8 us (44%)
  waiting for transfers between devices  24.9 us (24%)
  starting transfers between devices  20.8 us (20%)
  Pallas kernels  12.3 us (12%)
    all_to_all x1, blocking collectives, exchange(): return lax.all_to_all(rows, 'chip', split_axis=0, concat_axis=0, tiled=True)  35.9 us
    all_to_all x1, waiting for transfers between devices, exchange(): return lax.all_to_all(rows, 'chip', split_axis=0, concat_axis=0, tiled=True)  22.6 us
    all_to_all x1, starting transfers between devices, exchange(): return lax.all_to_all(rows, 'chip', split_axis=0, concat_axis=0, tiled=True)  18.9 us
    all_to_all x1, blocking collectives, local(): lax.all_to_all(partial, 'bl', split_axis=0, concat_axis=0, tiled=True)  9.89 us
    pallas_call x1, Pallas kernels, local(): pl.pallas_call(dft_kernel, in_specs=[hbm, hbm, hbm], out_specs=[hbm, vmem...  5.03 us
    pallas_call x1, Pallas kernels, local(): pl.pallas_call(relay_kernel, grid=(4,), in_specs=[smem, pl.BlockSpec((CAP...  4.31 us
    ppermute x1, waiting for transfers between devices, local(): other = lax.ppermute(sent, 'core', [(0, 1), (1, 0)])  2.31 us
  transfers between devices with their start and end apart: 2, of which 2 were waited for; matrix products, arithmetic and copies ran while one was open for 0% of the time, Pallas kernels for 4%

profile of v9, /device:TPU:6, one launch (start us, length us, event | category | flops | bytes accessed | tf_op | source)
XLA Modules:
  0.0 104.5 jit_solution(9965100052405089878)
XLA Ops:
  0.0 5.0 %dft.1 = (bf16[64,2,8,256]{3,2,1,0:T(8,128)(2,1)}, s32[1,384]{1,0:T(1,128)S(1)}) custom-call(s32[1,384]{1,0:T(1,128)} %bitcast.5, bf16[512,2048]{1,0:T(8,128)(2,1)} %bitcast.4, bf16[1024,768]{1,0:T(8,128)(2,1)} %constant.24.clone.wave_hbm), custom_call_target="tpu_custom_call" | custom-call | tf_op jit(solution)/shard_map/dft/pallas_call | solution.py:213
  5.0 0.0 copy-start
  5.1 18.9 %all-to-all-start = ((bf16[64,2,8,256]{3,2,1,0:T(8,128)(2,1)}), bf16[64,2,8,256]{3,2,1,0:T(8,128)(2,1)S(1)}, u32[]{:S(2)}, u32[]{:S(2)}) async-start(bf16[64,2,8,256]{3,2,1,0:T(8,128)(2,1)} %get-tuple-element.13), calls=%async_computation | async-start | bytes 1048576 | tf_op jit(solution)/shard_map/all_to_all | solution.py:232
  24.0 4.3 %relay.1 = (bf16[64,32,256]{2,1,0:T(8,128)(2,1)S(1)}, bf16[64,32,256]{2,1,0:T(8,128)(2,1)}) custom-call(s32[1]{0:T(128)} %bitcast.2.core_ref, bf16[4,128,2,4,256]{4,3,2,1,0:T(4,128)(2,1)} %fac_ref), custom_call_target="tpu_custom_call" | custom-call | tf_op jit(solution)/shard_map/relay/pallas_call | solution.py:238
  28.3 1.9 %collective-permute-start = (bf16[64,32,256]{2,1,0:T(8,128)(2,1)}, bf16[64,32,256]{2,1,0:T(8,128)(2,1)S(1)}, u32[]{:S(2)}, u32[]{:S(2)}) collective-permute-start(bf16[64,32,256]{2,1,0:T(8,128)(2,1)} %get-tuple-element.16), channel_id=1, source_target_pairs={{0,4},{4,0},{1,5},{5,1},{2,6},{6,2},{3,7},{7,3},{8,12},{12,8},{9,1... | collective-permute-start | bytes 3145736 | tf_op jit(solution)/shard_map/ppermute | solution.py:248
  30.2 0.1 iota_add_fusion
  30.3 0.1 add.46
  30.4 0.0 copy-done
  30.4 0.3 fusion
  30.7 2.3 %collective-permute-done.other_ref = bf16[64,32,256]{2,1,0:T(8,128)(2,1)S(1)} collective-permute-done((bf16[64,32,256]{2,1,0:T(8,128)(2,1)}, bf16[64,32,256]{2,1,0:T(8,128)(2,1)S(1)}, u32[]{:S(2)}, u32[]{:S(2)}) %collective-permute-start) | collective-permute-done | bytes 1048608 | tf_op jit(solution)/shard_map/ppermute | solution.py:248
  33.1 22.6 %all-to-all-done.vis_ref = bf16[64,2,8,256]{3,2,1,0:T(8,128)(2,1)S(1)} async-done(((bf16[64,2,8,256]{3,2,1,0:T(8,128)(2,1)}), bf16[64,2,8,256]{3,2,1,0:T(8,128)(2,1)S(1)}, u32[]{:S(2)}, u32[]{:S(2)}) %all-to-all-start) | async-done | bytes 524320 | tf_op jit(solution)/shard_map/all_to_all | solution.py:232
  55.7 0.9 coef.1
  56.6 9.9 %all_to_all.15.part_ref = f32[4,32,128]{2,1,0:T(8,128)S(1)} all-to-all(f32[4,32,128]{2,1,0:T(8,128)S(1)} %get-tuple-element.17), channel_id=1, replica_groups=mesh['chip'=64,'core'=2,'bl'=4] {'bl'}, dimensions={0} | all-to-all | bytes 131072 | tf_op jit(solution)/shard_map/all_to_all | solution.py:269
  66.5 0.9 synth.1
  67.4 35.9 %all_to_all.16.slots_ref = bf16[64,2,8,256]{3,2,1,0:T(8,128)(2,1)S(1)} all-to-all(bf16[64,2,8,256]{3,2,1,0:T(8,128)(2,1)S(1)} %synth.1), channel_id=1, replica_groups=mesh['chip'=64,'core'=2,'bl'=4] {'chip'}, dimensions={0} | all-to-all | bytes 1048576 | tf_op jit(solution)/shard_map/all_to_all | solution.py:232
  103.3 1.2 %final.1 = bf16[2,256,384]{2,1,0:T(8,128)(2,1)} custom-call(s32[1,384]{1,0:T(1,128)S(1)} %get-tuple-element.12.target_ref, bf16[64,2,8,256]{3,2,1,0:T(8,128)(2,1)S(1)} %all_to_all.16.slots_ref), custom_call_target="tpu_custom_call" | custom-call | tf_op jit(solution)/shard_map/final/pallas_call | solution.py:278
  (5 shorter events, 0.0 us)
Async XLA Ops:
  5.0 25.4 %copy-start = (s32[384,128]{1,0:T(8,128)S(1)}, s32[384,128]{1,0:T(8,128)}, u32[]{:S(2)}) copy-start(s32[384,128]{1,0:T(8,128)} %param.7) | copy-start | bytes 589828
  5.1 50.6 %all-to-all-start = ((bf16[64,2,8,256]{3,2,1,0:T(8,128)(2,1)}), bf16[64,2,8,256]{3,2,1,0:T(8,128)(2,1)S(1)}, u32[]{:S(2)}, u32[]{:S(2)}) async-start(bf16[64,2,8,256]{3,2,1,0:T(8,128)(2,1)} %get-tuple-element.13), calls=%async_computation | async-start | bytes 1048576 | tf_op jit(solution)/shard_map/all_to_all | solution.py:232
  28.3 4.8 %collective-permute-start = (bf16[64,32,256]{2,1,0:T(8,128)(2,1)}, bf16[64,32,256]{2,1,0:T(8,128)(2,1)S(1)}, u32[]{:S(2)}, u32[]{:S(2)}) collective-permute-start(bf16[64,32,256]{2,1,0:T(8,128)(2,1)} %get-tuple-element.16), channel_id=1, source_target_pairs={{0,4},{4,0},{1,5},{5,1},{2,6},{6,2},{3,7},{7,3},{8,12},{12,8},{9,1... | collective-permute-start | bytes 3145736 | tf_op jit(solution)/shard_map/ppermute | solution.py:248
